TPU v7x, 256 devices: a whole 4x4x8 slice. The times are simulated.
256 devices in a mesh: tm: 32 (over y, z_hi, core), fiber: 8 (over x, z_lo).
Axes of the slice: x: 4, y: 4, z: 8 (z_hi: 4, z_lo: 2; z = z_hi * 2 + z_lo), core: 2. Of those that a mesh axis runs over, the one named last changes fastest.
Arguments:
- waveform: bfloat16 [4096, 65536], P('fiber', 'tm'), may hold values from -6 to 6
- filters: bfloat16 [512, 256], replicated, may hold values from -0.25 to 0.25
- channel_section: int32 [4096], replicated, may hold values from 0 to 127, never falling along the last dimension, each value on 1 to 64 neighbouring positions
- section_bank: int32 [128, 8], replicated, may hold values from 0 to 1
- conv_bank: bfloat16 [2, 8, 3, 3, 32, 32], P(None, 'fiber'), may hold values from -0.375 to 0.375
Outputs:
- events: bfloat16 [4096, 256, 512], P('tm', 'fiber')
Inputs may be any that keep to these rules, and one draw needn't show every extreme that they name: `channel_section`: never falls along the channels; every section has 1 to 64 channels.
All inputs are finite; a program needn't handle non-finite values.
Results may differ from a plain program's by a relative error of at most 0.005.
Values may be sent and summed in bfloat16 or wider, within the bound.
No kernel may reach another device: no remote copies, remote signals or barrier semaphores. Data moves between devices by JAX's collectives and lax.ppermute only.
A program may use at most 128 MiB of HBM per device.

v0:
```python
import jax
import jax.numpy as jnp
from jax import lax
from jax.experimental import pallas as pl
from jax.experimental.pallas import tpu as pltpu
from jax.sharding import PartitionSpec as P

HOP = 128
GW = 32
AXES = ("tm", "fiber")
TURN = 0


PLACES = [(x, y, z, c) for x in range(4) for y in range(4) for z in range(8) for c in range(2)]


def flat(x, y, z, c):
    return ((y * 4 + z // 2) * 2 + c) * 8 + x * 2 + z % 2


def spot(x, y, late, odd, b, core, early):
    return flat((x - y + TURN - early) % 4, x, 4 * odd + 2 * b + (late ^ odd), core)


def bulk_route(step):
    pairs = []
    for x, y, z, c in PLACES:
        pair, odd = z // 2, z % 2
        late = 0 if pair in (0, 3) else 1
        there = spot(x, y, late, odd, step ^ (pair // 2), c, int(pair == 3))
        pairs.append((flat(x, y, z, c), there))
    return pairs


OTHER_CORE = [(i, i ^ 1) for i in range(32)]


def flip_kernel(taps_ref, out_ref):
    out_ref[...] = taps_ref[...].T


def filter_kernel(where_ref, first_ref, second_ref, other_ref, taps_ref, out_ref, seq_ref, early_ref):
    first, core, keep = where_ref[0], where_ref[1], where_ref[2]
    size = first_ref.shape[1]
    seq_ref[:, 80:96, :] = jnp.zeros((size, 16, HOP), jnp.bfloat16)
    early_ref[...] = jnp.zeros(early_ref.shape, jnp.float32)

    def apply(frames):
        return lax.dot_general(
            taps_ref[...], frames, (((1,), (1,)), ((), ())), preferred_element_type=jnp.float32
        ).astype(jnp.bfloat16)

    for base in range(0, size, 16):
        chans = min(16, size - base)
        rows = slice(base, base + chans)
        parts = (first_ref[core, rows], other_ref[0, rows], second_ref[core, rows], other_ref[1, rows])
        for j, part in enumerate(parts):
            at = (first ^ (j >> 1)) * 48 + (core ^ (j & 1)) * 16
            seq_ref[rows, pl.ds(pl.multiple_of(at, 16), 16), :] = part
        seq_ref[rows, 32:48, :] = seq_ref[rows, 48:64, :] * keep.astype(jnp.bfloat16)
        columns = []
        for k in range(4):
            runs = [seq_ref[rows, s + k : s + k + 32, :] for s in (0, 48)]
            columns.append(jnp.concatenate(runs, axis=1).reshape(chans * 64, HOP))
        feats = apply(jnp.concatenate(columns, axis=1))
        for g in range(8):
            for p in range(chans // 2):
                out_ref[g, base // 2 + p] = feats[
                    g * GW : (g + 1) * GW, p * 128 : (p + 1) * 128
                ]
        for c in range(chans):
            pair, side = (base + c) // 2, c % 2
            at = 128 * (pair // 21) + 64 * side + 3 * (pair % 21)
            head = seq_ref[base + c, 0:3, :].astype(jnp.float32)
            for k in range(1, 4):
                early_ref[at + 3 - k : at + 3, k * HOP : (k + 1) * HOP] = head[:k]
    feats = apply(early_ref[...].astype(jnp.bfloat16))
    for g in range(8):
        for h in range(2):
            out_ref[g, size // 2 + h] = feats[g * GW : (g + 1) * GW, h * 128 : (h + 1) * 128]


def weight_kernel(flag_ref, kern_ref, out_ref, base_ref):
    block = pl.program_id(0)

    @pl.when(block == 0)
    def _():
        r = lax.broadcasted_iota(jnp.int32, (288, 960), 0)
        k = lax.broadcasted_iota(jnp.int32, (288, 960), 1)
        lag = k - r - 224 * ((r >= 96).astype(jnp.int32) + (r >= 192).astype(jnp.int32))
        for c in range(8):
            spread = jnp.where(lag == 32 * c, 1.0, 0.0).astype(jnp.bfloat16)
            base_ref[c] = jnp.dot(kern_ref[...], spread, preferred_element_type=jnp.float32)

    k = lax.broadcasted_iota(jnp.int32, (1, 960), 1)
    k = k - 320 * ((k >= 320).astype(jnp.int32) + (k >= 640).astype(jnp.int32))
    for c in range(8):
        at = block * 8 + c
        low, high = flag_ref[1, at].astype(jnp.float32), flag_ref[2, at].astype(jnp.float32)
        mask = jnp.where(k < 32 * c + 32, low, jnp.where(k >= 32 * c + 64, high, 1.0))
        rows = base_ref[c, pl.ds(pl.multiple_of(flag_ref[0, at] * GW, GW), GW), :]
        out_ref[0, c * GW : (c + 1) * GW, :] = (rows * mask).astype(jnp.bfloat16)


def assemble(x_ref, load, pairs, sides, place):
    size = pairs * GW
    lane = lax.broadcasted_iota(jnp.int16, (size, 128), 1)
    v = [load(q).reshape(size, 128) for q in range(8)]
    near = [pltpu.roll(u, 32, 1) for u in v]
    far = [pltpu.roll(u, 96, 1) for u in v]
    zero = jnp.zeros((size, 128), jnp.bfloat16)
    for side in sides:
        outer, inner = (near, far) if side else (far, near)
        t = [
            jnp.where(
                lane < 32,
                outer[2 * m],
                jnp.where(lane < 96, inner[2 * m + 1], outer[(2 * m + 2) % 8]),
            )
            for m in range(4)
        ]
        back = [pltpu.roll(u, 1, 1) for u in t]
        ahead = [pltpu.roll(u, 127, 1) for u in t]
        for m in range(4):
            before = jnp.where(lane == 0, back[m - 1] if m else zero, back[m])
            after = jnp.where(lane == 127, ahead[m + 1] if m < 3 else zero, ahead[m])
            for e, u in enumerate((before, t[m], after)):
                for p in range(pairs):
                    x_ref[e, place(p, side), :, m * 128 : (m + 1) * 128] = u[
                        p * GW : (p + 1) * GW
                    ]


def multiply(w_ref, x_ref, row, out_ref):
    x = jnp.concatenate(
        [x_ref[e, pl.ds(row, 10)].reshape(10 * GW, 512) for e in range(3)], axis=0
    )
    res = jnp.dot(w_ref[0], x, preferred_element_type=jnp.float32)
    out_ref[...] = res.astype(jnp.bfloat16).reshape(8, GW, 512)


def place_early(late_ref, load, spread_ref):
    for h in range(2):
        rows = jnp.concatenate([load(q, h) for q in range(8)], axis=0)
        for j in range(0, 21, 7):
            res = jnp.dot(
                rows, spread_ref[:, j * 128 : (j + 7) * 128], preferred_element_type=jnp.float32
            ).astype(jnp.bfloat16)
            for k in range(7):
                for q in range(8):
                    late_ref[21 * h + j + k, (q + 7) % 8] = res[
                        q * GW : (q + 1) * GW, k * 128 : (k + 1) * 128
                    ]


def inner_kernel(slot_ref, recv_ref, spread_ref, w_ref, out_ref, side_ref, x_ref, late_ref):
    step = pl.program_id(0)

    @pl.when(step == 0)
    def _():
        place_early(late_ref, lambda q, h: recv_ref[slot_ref[q], 32 + h], spread_ref)

        @pl.loop(0, 8)
        def _(g):
            assemble(
                x_ref,
                lambda q: recv_ref[slot_ref[q], pl.ds(g * 4, 4)] + late_ref[pl.ds(g * 4, 4), q],
                4,
                (0, 1),
                lambda p, side: 8 * g + 2 * p + side,
            )

        for e in range(3):
            side_ref[e, 0:9] = x_ref[e, 0:9]
            side_ref[e, 9:18] = x_ref[e, 55:64]

    multiply(w_ref, x_ref, step * 8 + 7, out_ref)


def outer_kernel(slot_ref, recv_ref, spread_ref, side_ref, w_ref, done_ref, out_ref, x_ref, late_ref):
    step = pl.program_id(0)

    def group(g):
        at = 8 * g + 1 + 18 * (g // 4)
        assemble(
            x_ref,
            lambda q: recv_ref[slot_ref[q], pl.ds(g * 4, 4)] + late_ref[pl.ds(g * 4, 4), q],
            4,
            (0, 1),
            lambda p, side: at + 2 * p + side,
        )

    row = 8 * step + 2 * (step // 5)

    @pl.when(step == 0)
    def _():
        place_early(late_ref, lambda q, h: recv_ref[slot_ref[q], 33 + h], spread_ref)
        for e in range(3):
            x_ref[e, 33:51] = side_ref[e]
        assemble(
            x_ref,
            lambda q: recv_ref[slot_ref[q], 32] + late_ref[32, q],
            1,
            (0, 1),
            lambda p, side: 83 * side,
        )
        group(0)

    @pl.when(step < 7)
    def _():
        group(step + 1)
        multiply(w_ref, x_ref, row, out_ref)

    @pl.when(step >= 7)
    def _():
        multiply(w_ref, x_ref, row, out_ref)


def whole(*shape):
    return pl.BlockSpec(shape, lambda i, s: (0,) * len(shape))


VMEM = pl.BlockSpec(memory_space=pltpu.VMEM)
SMEM = pl.BlockSpec(memory_space=pltpu.SMEM)


def shards(waveform, filters, channel_section, section_bank, conv_bank):
    tm, fiber = lax.axis_index("tm"), lax.axis_index("fiber")
    y, zh, core, x, z0 = tm >> 3, (tm >> 1) & 3, tm & 1, fiber >> 1, fiber & 1
    z2, z1 = zh >> 1, zh & 1
    late = z0 ^ z2
    first = 1 ^ z1 ^ late

    def send(part, perm, axes=AXES):
        return lax.ppermute(part, axes, perm)

    got = ([], [])
    for step in (0, 1):
        rows = lax.dynamic_slice_in_dim(waveform, 256 * (step ^ z2), 256, 0)
        part = rows.reshape(2, 128, 16, HOP)[:, 32:96]
        got[0].append(send(part, bulk_route(step)))
    up = [(i, i + 1) for i in range(7)]
    row_low = send(waveform[511:], up, "fiber")
    row_high = send(waveform[:1], [(j, i) for i, j in up], "fiber")
    wave, row_low, row_high = lax.optimization_barrier((waveform, row_low, row_high))
    sides = [row_low] + [wave[i : i + 1] for i in (128, 127, 256, 255, 384, 383)] + [row_high]
    sides = jnp.concatenate(sides, axis=0).reshape(4, 2, 16, HOP)
    for step in (0, 1):
        rows = lax.dynamic_slice_in_dim(wave, 256 * (step ^ z2), 256, 0)
        rows = rows.reshape(2, 128, 16, HOP)
        extra = lax.dynamic_slice_in_dim(sides, 2 * (step ^ z2), 2, 0)
        part = jnp.concatenate([rows[:, :32], rows[:, 96:], extra], axis=1)
        got[1].append(send(part, bulk_route(step)))

    taps = pl.pallas_call(
        flip_kernel,
        out_shape=jax.ShapeDtypeStruct((256, 512), jnp.bfloat16),
        cost_estimate=pl.CostEstimate(flops=0, bytes_accessed=1 << 19, transcendentals=0),
        name="flip",
    )(filters)

    keep = jnp.where((late == 0) & (((y - x + TURN) & 3) == 0), 0, 1)
    where = jnp.stack([first, core, keep]).astype(jnp.int32)
    recv = []
    for half in (0, 1):
        size = 66 if half else 64
        theirs = [lax.dynamic_index_in_dim(g, 1 - core, 0, False) for g in got[half]]
        other = send(jnp.stack(theirs), OTHER_CORE, "tm")
        feats = pl.pallas_call(
            filter_kernel,
            out_shape=jax.ShapeDtypeStruct((8, size // 2 + 2, GW, 128), jnp.bfloat16),
            in_specs=[SMEM] + [VMEM] * 4,
            out_specs=VMEM,
            scratch_shapes=[
                pltpu.VMEM((size, 96, HOP), jnp.bfloat16),
                pltpu.VMEM((256, 512), jnp.float32),
            ],
            cost_estimate=pl.CostEstimate(
                flops=size * 2 * 64 * 512 * 256, bytes_accessed=size * 49152, transcendentals=0
            ),
            name="filterbank",
        )(where, *got[half], other, taps)
        recv.append(lax.all_to_all(feats, "fiber", 0, 0, tiled=True))

    edge = jnp.array([-1], jnp.int32)
    sec = lax.dynamic_slice_in_dim(
        jnp.concatenate([edge, channel_section, edge]), tm * 128, 130, 0
    )
    middle = sec[1:-1]
    table = lax.dynamic_slice_in_dim(section_bank, fiber, 1, 1)
    onehot = (middle[:, None] == jnp.arange(table.shape[0], dtype=jnp.int32)[None, :]).astype(
        jnp.int32
    )
    choose = jnp.sum(onehot * table[:, 0][None, :], axis=1)
    flags = jnp.stack([choose, sec[:-2] == middle, sec[2:] == middle]).astype(jnp.int32)
    kern = conv_bank[:, 0].transpose(0, 3, 2, 1, 4).reshape(64, 288)
    weights = pl.pallas_call(
        weight_kernel,
        out_shape=jax.ShapeDtypeStruct((16, 256, 960), jnp.bfloat16),
        grid_spec=pltpu.PrefetchScalarGridSpec(
            num_scalar_prefetch=1,
            grid=(16,),
            in_specs=[whole(64, 288)],
            out_specs=pl.BlockSpec((1, 256, 960), lambda i, s: (i, 0, 0)),
            scratch_shapes=[pltpu.VMEM((8, 64, 960), jnp.float32)],
        ),
        cost_estimate=pl.CostEstimate(
            flops=8 * 2 * 64 * 288 * 960, bytes_accessed=8 << 20, transcendentals=0
        ),
        name="weights",
    )(flags, kern)

    q = jnp.arange(8, dtype=jnp.int32)
    slot = (2 * ((y + TURN - (q >> 1)) & 3) + ((q & 1) ^ z2)).astype(jnp.int32)
    at = jnp.arange(21 * 128, dtype=jnp.int32)
    source = jnp.where(at % 64 >= 61, (at % 128) // 64 * 64 + 3 * (at // 128) + at % 64 - 61, -1)
    spread = (jnp.arange(128, dtype=jnp.int32)[:, None] == source[None, :]).astype(jnp.bfloat16)
    late_rows = pltpu.VMEM((42, 8, GW, 128), jnp.bfloat16)
    part, side = pl.pallas_call(
        inner_kernel,
        out_shape=(
            jax.ShapeDtypeStruct((128, GW, 512), jnp.bfloat16),
            jax.ShapeDtypeStruct((3, 18, GW, 512), jnp.bfloat16),
        ),
        grid_spec=pltpu.PrefetchScalarGridSpec(
            num_scalar_prefetch=1,
            grid=(6,),
            in_specs=[
                whole(8, 34, GW, 128),
                whole(128, 21 * 128),
                pl.BlockSpec((1, 256, 960), lambda i, s: (i + 5, 0, 0)),
            ],
            out_specs=(
                pl.BlockSpec((8, GW, 512), lambda i, s: (i + 5, 0, 0)),
                whole(3, 18, GW, 512),
            ),
            scratch_shapes=[pltpu.VMEM((3, 64, GW, 512), jnp.bfloat16), late_rows],
        ),
        cost_estimate=pl.CostEstimate(
            flops=6 * 2 * 256 * 960 * 512, bytes_accessed=8 << 20, transcendentals=0
        ),
        name="conv_inner",
    )(slot, recv[0], spread, weights)
    return pl.pallas_call(
        outer_kernel,
        out_shape=jax.ShapeDtypeStruct((128, GW, 512), jnp.bfloat16),
        grid_spec=pltpu.PrefetchScalarGridSpec(
            num_scalar_prefetch=1,
            grid=(10,),
            in_specs=[
                whole(8, 35, GW, 128),
                whole(128, 21 * 128),
                whole(3, 18, GW, 512),
                pl.BlockSpec((1, 256, 960), lambda i, s: (i + 6 * (i // 5), 0, 0)),
                pl.BlockSpec(memory_space=pl.ANY),
            ],
            out_specs=pl.BlockSpec((8, GW, 512), lambda i, s: (i + 6 * (i // 5), 0, 0)),
            scratch_shapes=[pltpu.VMEM((3, 84, GW, 512), jnp.bfloat16), late_rows],
        ),
        input_output_aliases={5: 0},
        cost_estimate=pl.CostEstimate(
            flops=10 * 2 * 256 * 960 * 512, bytes_accessed=8 << 20, transcendentals=0
        ),
        name="conv_outer",
    )(slot, recv[1], spread, side, weights, part)


def solution(mesh):
    placed = (P("fiber", "tm"), P(), P(), P(), P(None, "fiber", None, None, None, None))

    return jax.shard_map(
        shards, mesh=mesh, in_specs=placed, out_specs=P("tm", "fiber", None), check_vma=False
    )
```

profile of v0, /device:TPU:16, one launch (start us, length us, event | category | flops | bytes accessed | tf_op | source)
XLA Modules:
  0.0 169.8 jit_solution(8960477193044300101)
XLA Ops:
  0.0 0.0 copy-start
  0.0 1.7 dynamic-slice_bitcast_fusion
  1.7 0.2 copy.19
  2.0 5.6 %collective-permute-start.6 = (bf16[2,64,16,128]{3,2,1,0:T(8,128)(2,1)S(1)}, bf16[2,64,16,128]{3,2,1,0:T(8,128)(2,1)S(1)}, u32[]{:S(2)}, u32[]{:S(2)}) collective-permute-start(bf16[2,64,16,128]{3,2,1,0:T(8,128)(2,1)S(1)} %slice.73), channel_id=1, source_target_pairs={{0,16},{8,24},{1,49},{9,57},{16,17},{24,25},{17,48},{25,56},{32,1}... | collective-permute-start | bytes 1572872 | tf_op jit(solution)/shard_map/ppermute | solution.py:235
  7.6 0.2 copy.18
  7.8 5.1 %collective-permute-start.5 = (bf16[2,64,16,128]{3,2,1,0:T(8,128)(2,1)S(1)}, bf16[2,64,16,128]{3,2,1,0:T(8,128)(2,1)S(1)}, u32[]{:S(2)}, u32[]{:S(2)}) collective-permute-start(bf16[2,64,16,128]{3,2,1,0:T(8,128)(2,1)S(1)} %slice.72), channel_id=1, source_target_pairs={{0,0},{8,8},{1,33},{9,41},{16,1},{24,9},{17,32},{25,40},{32,17},{4... | collective-permute-start | bytes 1572872 | tf_op jit(solution)/shard_map/ppermute | solution.py:235
  12.9 10.5 %collective-permute-done.6.second_ref = bf16[2,64,16,128]{3,2,1,0:T(8,128)(2,1)S(1)} collective-permute-done((bf16[2,64,16,128]{3,2,1,0:T(8,128)(2,1)S(1)}, bf16[2,64,16,128]{3,2,1,0:T(8,128)(2,1)S(1)}, u32[]{:S(2)}, u32[]{:S(2)}) %collective-permute-start.6) | collective-permute-done | bytes 524320 | tf_op jit(solution)/shard_map/ppermute | solution.py:235
  23.5 0.0 copy-start.5
  23.5 10.5 %collective-permute-done.5.first_ref = bf16[2,64,16,128]{3,2,1,0:T(8,128)(2,1)S(1)} collective-permute-done((bf16[2,64,16,128]{3,2,1,0:T(8,128)(2,1)S(1)}, bf16[2,64,16,128]{3,2,1,0:T(8,128)(2,1)S(1)}, u32[]{:S(2)}, u32[]{:S(2)}) %collective-permute-start.5) | collective-permute-done | bytes 524320 | tf_op jit(solution)/shard_map/ppermute | solution.py:235
  34.0 0.1 pad_maximum_fusion.3
  34.1 0.1 collective-permute-start.7
  34.2 1.8 %flip.1.taps_ref = bf16[256,512]{1,0:T(8,128)(2,1)} custom-call(bf16[512,256]{1,0:T(8,128)(2,1)} %taps_ref.1), custom_call_target="tpu_custom_call" | custom-call | bytes 524288 | tf_op jit(solution)/shard_map/flip/pallas_call | solution.py:255
  36.0 0.6 pad_add_fusion.1.where_ref
  36.6 0.0 collective-permute-done.7.other_ref
  36.6 0.0 copy-done.5
  36.6 0.0 copy-done.6
  36.6 0.0 copy-start.7
  36.6 0.8 copy-done.7
  37.4 4.4 %filterbank.3 = bf16[8,34,32,128]{3,2,1,0:T(8,128)(2,1)} custom-call(s32[3]{0:T(128)} %pad_add_fusion.1.where_ref, bf16[2,64,16,128]{3,2,1,0:T(8,128)(2,1)} %copy-done.6, bf16[2,64,16,128]{3,2,1,0:T(8,128)(2,1)} %copy-done.5, bf16[2,64,16,128]{3,2,1,0:T(8,128)(2,1)} %copy-done.7, bf16[256,512]{1,0:T(8,128)(2,1)} %flip.1.taps_ref), custom_call_target="tpu_custom_call" | custom-call | flops 1073741824 | bytes 3145728 | tf_op jit(solution)/shard_map/filterbank/pallas_call | solution.py:269
  41.7 4.1 %all-to-all-start.1 = ((bf16[8,34,32,128]{3,2,1,0:T(8,128)(2,1)}), bf16[8,34,32,128]{3,2,1,0:T(8,128)(2,1)S(1)}, u32[]{:S(2)}, u32[]{:S(2)}) async-start(bf16[8,34,32,128]{3,2,1,0:T(8,128)(2,1)} %filterbank.3), calls=%async_computation.1 | async-start | bytes 4456448 | tf_op jit(solution)/shard_map/all_to_all | solution.py:283
  45.8 0.8 fusion.29
  46.6 1.3 collective-permute-start.1
  47.9 4.6 %collective-permute-start = (bf16[1,2048]{1,0:T(2,128)(2,1)S(1)}, bf16[1,2048]{1,0:T(2,128)(2,1)S(1)}, u32[]{:S(2)}, u32[]{:S(2)}) collective-permute-start(bf16[1,2048]{1,0:T(2,128)(2,1)S(1)} %get-tuple-element.26), channel_id=1, source_target_pairs={{0,1},{1,2},{2,3},{3,4},{4,5},{5,6},{6,7},{8,9},{9,10},{10,11},{11... | collective-permute-start | bytes 12296 | tf_op jit(solution)/shard_map/ppermute | solution.py:235
  52.5 21.4 %collective-permute-done.1 = bf16[1,2048]{1,0:T(2,128)(2,1)S(1)} collective-permute-done((bf16[1,2048]{1,0:T(2,128)(2,1)S(1)}, bf16[1,2048]{1,0:T(2,128)(2,1)S(1)}, u32[]{:S(2)}, u32[]{:S(2)}) %collective-permute-start.1) | collective-permute-done | bytes 4128 | tf_op jit(solution)/shard_map/ppermute | solution.py:235
  73.8 0.0 collective-permute-done
  73.8 0.9 fusion.28
  74.7 0.1 concatenate.12
  74.9 1.7 dynamic-slice_bitcast_fusion.2
  76.5 0.2 copy.17
  76.8 0.1 pad_maximum_fusion.1
  76.9 7.1 %collective-permute-start.3 = (bf16[2,66,16,128]{3,2,1,0:T(8,128)(2,1)S(1)}, bf16[2,66,16,128]{3,2,1,0:T(8,128)(2,1)S(1)}, u32[]{:S(2)}, u32[]{:S(2)}) collective-permute-start(bf16[2,66,16,128]{3,2,1,0:T(8,128)(2,1)S(1)} %pad_maximum_fusion.1), channel_id=1, source_target_pairs={{0,16},{8,24},{1,49},{9,57},{16,17},{24,25},{17,48},{25,56},{32,1}... | collective-permute-start | bytes 1622024 | tf_op jit(solution)/shard_map/ppermute | solution.py:235
  84.1 0.2 copy.15
  84.3 0.1 pad_maximum_fusion
  84.4 4.6 %collective-permute-start.2 = (bf16[2,66,16,128]{3,2,1,0:T(8,128)(2,1)S(1)}, bf16[2,66,16,128]{3,2,1,0:T(8,128)(2,1)S(1)}, u32[]{:S(2)}, u32[]{:S(2)}) collective-permute-start(bf16[2,66,16,128]{3,2,1,0:T(8,128)(2,1)S(1)} %pad_maximum_fusion), channel_id=1, source_target_pairs={{0,0},{8,8},{1,33},{9,41},{16,1},{24,9},{17,32},{25,40},{32,17},{4... | collective-permute-start | bytes 1622024 | tf_op jit(solution)/shard_map/ppermute | solution.py:235
  89.1 8.5 %collective-permute-done.3.second_ref = bf16[2,66,16,128]{3,2,1,0:T(8,128)(2,1)S(1)} collective-permute-done((bf16[2,66,16,128]{3,2,1,0:T(8,128)(2,1)S(1)}, bf16[2,66,16,128]{3,2,1,0:T(8,128)(2,1)S(1)}, u32[]{:S(2)}, u32[]{:S(2)}) %collective-permute-start.3) | collective-permute-done | bytes 540704 | tf_op jit(solution)/shard_map/ppermute | solution.py:235
  97.6 10.3 %collective-permute-done.2.first_ref = bf16[2,66,16,128]{3,2,1,0:T(8,128)(2,1)S(1)} collective-permute-done((bf16[2,66,16,128]{3,2,1,0:T(8,128)(2,1)S(1)}, bf16[2,66,16,128]{3,2,1,0:T(8,128)(2,1)S(1)}, u32[]{:S(2)}, u32[]{:S(2)}) %collective-permute-start.2) | collective-permute-done | bytes 540704 | tf_op jit(solution)/shard_map/ppermute | solution.py:235
  107.9 0.1 pad_maximum_fusion.2
  107.9 0.1 collective-permute-start.4
  108.0 2.1 %collective-permute-done.4.other_ref = bf16[2,66,16,128]{3,2,1,0:T(8,128)(2,1)} collective-permute-done((bf16[2,66,16,128]{3,2,1,0:T(8,128)(2,1)S(1)}, bf16[2,66,16,128]{3,2,1,0:T(8,128)(2,1)}, u32[]{:S(2)}, u32[]{:S(2)}) %collective-permute-start.4) | collective-permute-done | bytes 540704 | tf_op jit(solution)/shard_map/ppermute | solution.py:235
  110.1 0.0 copy-done.3
  110.1 0.0 copy-done.4
  110.1 4.6 %filterbank.2 = bf16[8,35,32,128]{3,2,1,0:T(8,128)(2,1)} custom-call(s32[3]{0:T(128)} %pad_add_fusion.1.where_ref, bf16[2,66,16,128]{3,2,1,0:T(8,128)(2,1)} %copy-done.4, bf16[2,66,16,128]{3,2,1,0:T(8,128)(2,1)} %copy-done.3, bf16[2,66,16,128]{3,2,1,0:T(8,128)(2,1)} %collective-permute-done.4.other_ref, bf16[256,512]{1,0:T(8,128)(2,1)} %flip.1.taps_ref), custom_call_target="tpu_custom_call" | custom-call | flops 1107296256 | bytes 3244032 | tf_op jit(solution)/shard_map/filterbank/pallas_call | solution.py:269
  114.7 0.0 all-to-all-done.1.recv_ref
  114.7 0.0 copy-start.2
  114.7 1.4 copy-done.2
  116.1 8.8 %all-to-all-start = ((bf16[8,35,32,128]{3,2,1,0:T(8,128)(2,1)}), bf16[8,35,32,128]{3,2,1,0:T(8,128)(2,1)S(1)}, u32[]{:S(2)}, u32[]{:S(2)}) async-start(bf16[8,35,32,128]{3,2,1,0:T(8,128)(2,1)} %filterbank.2), calls=%async_computation | async-start | bytes 4587520 | tf_op jit(solution)/shard_map/all_to_all | solution.py:283
  124.9 0.0 copy-done.9
  124.9 0.1 concatenate.15
  125.0 0.1 dynamic_slice.48
  125.1 0.1 slice.65
  125.2 0.0 copy-done.8
  125.2 0.1 copy.13
  125.3 0.8 reshape.77.kern_ref
  126.1 0.0 copy-done
  126.1 0.2 select_reduce_fusion
  126.2 0.1 fusion.25
  126.3 0.6 pad_add_fusion.flag_ref
  126.9 9.6 %weights.1.w_ref = bf16[16,256,960]{2,1,0:T(8,128)(2,1)} custom-call(s32[3,128]{1,0:T(4,128)} %pad_add_fusion.flag_ref, bf16[64,288]{1,0:T(8,128)(2,1)} %reshape.77.kern_ref), custom_call_target="tpu_custom_call" | custom-call | flops 283115520 | bytes 8388608 | tf_op jit(solution)/shard_map/weights/pallas_call | solution.py:297
  136.5 0.6 xor_add_fusion.slot_ref
  137.1 1.0 fusion.spread_ref
  138.1 12.0 %conv_inner.1 = (bf16[128,32,512]{2,1,0:T(8,128)(2,1)}, bf16[3,18,32,512]{3,2,1,0:T(8,128)(2,1)}) custom-call(s32[8]{0:T(128)} %xor_add_fusion.slot_ref, bf16[8,34,32,128]{3,2,1,0:T(8,128)(2,1)} %copy-done.2, bf16[128,2688]{1,0:T(8,128)(2,1)} %fusion.spread_ref, bf16[16,256,960]{2,1,0:T(8,128)(2,1)} %weights.1.w_ref), custom_call_target="tpu_custom_call" | custom-call | flops 1509949440 | bytes 8388608 | tf_op jit(solution)/shard_map/conv_inner/pallas_call | solution.py:319
  150.1 4.2 %all-to-all-done.recv_ref = bf16[8,35,32,128]{3,2,1,0:T(8,128)(2,1)S(1)} async-done(((bf16[8,35,32,128]{3,2,1,0:T(8,128)(2,1)}), bf16[8,35,32,128]{3,2,1,0:T(8,128)(2,1)S(1)}, u32[]{:S(2)}, u32[]{:S(2)}) %all-to-all-start) | async-done | bytes 2293792 | tf_op jit(solution)/shard_map/all_to_all | solution.py:283
  154.3 1.5 copy-done.1
  155.8 14.0 %conv_outer.1 = bf16[128,32,512]{2,1,0:T(8,128)(2,1)} custom-call(s32[8]{0:T(128)} %xor_add_fusion.slot_ref, bf16[8,35,32,128]{3,2,1,0:T(8,128)(2,1)} %copy-done.1, bf16[128,2688]{1,0:T(8,128)(2,1)} %fusion.spread_ref, bf16[3,18,32,512]{3,2,1,0:T(8,128)(2,1)} %get-tuple-element.13.side_ref, ...), custom_call_target="tpu_custom_call", output_to_operand_aliasing={{}: (5, {})} | custom-call | flops 2516582400 | bytes 8388608 | tf_op jit(solution)/shard_map/conv_outer/pallas_call | solution.py:344
  (18 shorter events, 0.3 us)
Async XLA Ops:
  0.0 126.1 %copy-start = (s32[128,8]{0,1:T(8,128)S(1)}, s32[128,8]{0,1:T(8,128)}, u32[]{:S(2)}) copy-start(s32[128,8]{0,1:T(8,128)} %param.9) | copy-start | bytes 12292
  2.0 21.5 %collective-permute-start.6 = (bf16[2,64,16,128]{3,2,1,0:T(8,128)(2,1)S(1)}, bf16[2,64,16,128]{3,2,1,0:T(8,128)(2,1)S(1)}, u32[]{:S(2)}, u32[]{:S(2)}) collective-permute-start(bf16[2,64,16,128]{3,2,1,0:T(8,128)(2,1)S(1)} %slice.73), channel_id=1, source_target_pairs={{0,16},{8,24},{1,49},{9,57},{16,17},{24,25},{17,48},{25,56},{32,1}... | collective-permute-start | bytes 1572872 | tf_op jit(solution)/shard_map/ppermute | solution.py:235
  7.8 26.1 %collective-permute-start.5 = (bf16[2,64,16,128]{3,2,1,0:T(8,128)(2,1)S(1)}, bf16[2,64,16,128]{3,2,1,0:T(8,128)(2,1)S(1)}, u32[]{:S(2)}, u32[]{:S(2)}) collective-permute-start(bf16[2,64,16,128]{3,2,1,0:T(8,128)(2,1)S(1)} %slice.72), channel_id=1, source_target_pairs={{0,0},{8,8},{1,33},{9,41},{16,1},{24,9},{17,32},{25,40},{32,17},{4... | collective-permute-start | bytes 1572872 | tf_op jit(solution)/shard_map/ppermute | solution.py:235
  23.5 13.1 %copy-start.5 = (bf16[2,64,16,128]{3,2,1,0:T(8,128)(2,1)}, bf16[2,64,16,128]{3,2,1,0:T(8,128)(2,1)S(1)}, u32[]{:S(2)}) copy-start(bf16[2,64,16,128]{3,2,1,0:T(8,128)(2,1)S(1)} %collective-permute-done.6.second_ref) | copy-start | bytes 1572868
  34.0 2.6 %copy-start.6 = (bf16[2,64,16,128]{3,2,1,0:T(8,128)(2,1)}, bf16[2,64,16,128]{3,2,1,0:T(8,128)(2,1)S(1)}, u32[]{:S(2)}) copy-start(bf16[2,64,16,128]{3,2,1,0:T(8,128)(2,1)S(1)} %collective-permute-done.5.first_ref) | copy-start | bytes 1572868
  34.1 2.5 %collective-permute-start.7 = (bf16[2,64,16,128]{3,2,1,0:T(8,128)(2,1)S(1)}, bf16[2,64,16,128]{3,2,1,0:T(8,128)(2,1)S(1)}, u32[]{:S(2)}, u32[]{:S(2)}) collective-permute-start(bf16[2,64,16,128]{3,2,1,0:T(8,128)(2,1)S(1)} %pad_maximum_fusion.3), channel_id=1, source_target_pairs={{0,8},{8,0},{16,24},{24,16},{32,40},{40,32},{48,56},{56,48},{64,72... | collective-permute-start | bytes 1572872 | tf_op jit(solution)/shard_map/ppermute | solution.py:235
  36.6 0.8 copy-start.7
  41.7 72.9 %all-to-all-start.1 = ((bf16[8,34,32,128]{3,2,1,0:T(8,128)(2,1)}), bf16[8,34,32,128]{3,2,1,0:T(8,128)(2,1)S(1)}, u32[]{:S(2)}, u32[]{:S(2)}) async-start(bf16[8,34,32,128]{3,2,1,0:T(8,128)(2,1)} %filterbank.3), calls=%async_computation.1 | async-start | bytes 4456448 | tf_op jit(solution)/shard_map/all_to_all | solution.py:283
  46.6 27.3 %collective-permute-start.1 = (bf16[1,2048]{1,0:T(2,128)(2,1)S(1)}, bf16[1,2048]{1,0:T(2,128)(2,1)S(1)}, u32[]{:S(2)}, u32[]{:S(2)}) collective-permute-start(bf16[1,2048]{1,0:T(2,128)(2,1)S(1)} %get-tuple-element.25), channel_id=1, source_target_pairs={{1,0},{2,1},{3,2},{4,3},{5,4},{6,5},{7,6},{9,8},{10,9},{11,10},{12... | collective-permute-start | bytes 12296 | tf_op jit(solution)/shard_map/ppermute | solution.py:235
  47.9 26.0 %collective-permute-start = (bf16[1,2048]{1,0:T(2,128)(2,1)S(1)}, bf16[1,2048]{1,0:T(2,128)(2,1)S(1)}, u32[]{:S(2)}, u32[]{:S(2)}) collective-permute-start(bf16[1,2048]{1,0:T(2,128)(2,1)S(1)} %get-tuple-element.26), channel_id=1, source_target_pairs={{0,1},{1,2},{2,3},{3,4},{4,5},{5,6},{6,7},{8,9},{9,10},{10,11},{11... | collective-permute-start | bytes 12296 | tf_op jit(solution)/shard_map/ppermute | solution.py:235
  76.9 20.6 %collective-permute-start.3 = (bf16[2,66,16,128]{3,2,1,0:T(8,128)(2,1)S(1)}, bf16[2,66,16,128]{3,2,1,0:T(8,128)(2,1)S(1)}, u32[]{:S(2)}, u32[]{:S(2)}) collective-permute-start(bf16[2,66,16,128]{3,2,1,0:T(8,128)(2,1)S(1)} %pad_maximum_fusion.1), channel_id=1, source_target_pairs={{0,16},{8,24},{1,49},{9,57},{16,17},{24,25},{17,48},{25,56},{32,1}... | collective-permute-start | bytes 1622024 | tf_op jit(solution)/shard_map/ppermute | solution.py:235
  84.4 23.4 %collective-permute-start.2 = (bf16[2,66,16,128]{3,2,1,0:T(8,128)(2,1)S(1)}, bf16[2,66,16,128]{3,2,1,0:T(8,128)(2,1)S(1)}, u32[]{:S(2)}, u32[]{:S(2)}) collective-permute-start(bf16[2,66,16,128]{3,2,1,0:T(8,128)(2,1)S(1)} %pad_maximum_fusion), channel_id=1, source_target_pairs={{0,0},{8,8},{1,33},{9,41},{16,1},{24,9},{17,32},{25,40},{32,17},{4... | collective-permute-start | bytes 1622024 | tf_op jit(solution)/shard_map/ppermute | solution.py:235
  97.6 12.5 %copy-start.3 = (bf16[2,66,16,128]{3,2,1,0:T(8,128)(2,1)}, bf16[2,66,16,128]{3,2,1,0:T(8,128)(2,1)S(1)}, u32[]{:S(2)}) copy-start(bf16[2,66,16,128]{3,2,1,0:T(8,128)(2,1)S(1)} %collective-permute-done.3.second_ref) | copy-start | bytes 1622020
  107.9 2.2 %copy-start.4 = (bf16[2,66,16,128]{3,2,1,0:T(8,128)(2,1)}, bf16[2,66,16,128]{3,2,1,0:T(8,128)(2,1)S(1)}, u32[]{:S(2)}) copy-start(bf16[2,66,16,128]{3,2,1,0:T(8,128)(2,1)S(1)} %collective-permute-done.2.first_ref) | copy-start | bytes 1622020
  107.9 2.2 %collective-permute-start.4 = (bf16[2,66,16,128]{3,2,1,0:T(8,128)(2,1)S(1)}, bf16[2,66,16,128]{3,2,1,0:T(8,128)(2,1)}, u32[]{:S(2)}, u32[]{:S(2)}) collective-permute-start(bf16[2,66,16,128]{3,2,1,0:T(8,128)(2,1)S(1)} %pad_maximum_fusion.2), channel_id=1, source_target_pairs={{0,8},{8,0},{16,24},{24,16},{32,40},{40,32},{48,56},{56,48},{64,72... | collective-permute-start | bytes 1622024 | tf_op jit(solution)/shard_map/ppermute | solution.py:235
  114.7 10.3 %copy-start.9 = (s32[4096]{0:T(1024)S(1)}, s32[4096]{0:T(1024)}, u32[]{:S(2)}) copy-start(s32[4096]{0:T(1024)} %param.8) | copy-start | bytes 49156
  114.7 10.5 %copy-start.8 = (bf16[2,1,3,3,32,32]{5,4,3,2,1,0:T(8,128)(2,1)S(1)}, bf16[2,1,3,3,32,32]{5,4,3,2,1,0:T(8,128)(2,1)}, u32[]{:S(2)}) copy-start(bf16[2,1,3,3,32,32]{5,4,3,2,1,0:T(8,128)(2,1)} %param.10) | copy-start | bytes 110596
  114.7 1.5 copy-start.2
  116.1 38.2 %all-to-all-start = ((bf16[8,35,32,128]{3,2,1,0:T(8,128)(2,1)}), bf16[8,35,32,128]{3,2,1,0:T(8,128)(2,1)S(1)}, u32[]{:S(2)}, u32[]{:S(2)}) async-start(bf16[8,35,32,128]{3,2,1,0:T(8,128)(2,1)} %filterbank.2), calls=%async_computation | async-start | bytes 4587520 | tf_op jit(solution)/shard_map/all_to_all | solution.py:283
  154.3 1.5 copy-start.1
where the time goes:
time: 173 us; the launch traced here: 170 us
  waiting for transfers between devices  67.4 us (39%)
  Pallas kernels  46.3 us (27%)
  starting transfers between devices  41.4 us (24%)
  local copies, waits for them, and re-layouts  11.1 us (6%)
  other arithmetic  3.3 us (2%)
    ppermute x8, waiting for transfers between devices, send(): return lax.ppermute(part, axes, perm)  63.2 us
    ppermute x8, starting transfers between devices, send(): return lax.ppermute(part, axes, perm)  28.5 us
    pallas_call x1, Pallas kernels, shards(): pl.pallas_call(outer_kernel, out_shape=jax.ShapeDtypeStruct((128, GW, 512...  14 us
    all_to_all x2, starting transfers between devices, shards(): recv.append(lax.all_to_all(feats, 'fiber', 0, 0, tiled=True))  12.9 us
    pallas_call x1, Pallas kernels, shards(): pl.pallas_call(inner_kernel, out_shape=(jax.ShapeDtypeStruct((128, GW, 51...  12 us
    pallas_call x1, Pallas kernels, shards(): pl.pallas_call(weight_kernel, out_shape=jax.ShapeDtypeStruct((16, 256, 96...  9.55 us
    pallas_call x2, Pallas kernels, shards(): pl.pallas_call(filter_kernel, out_shape=jax.ShapeDtypeStruct((8, size //...  8.91 us
    unnamed x27, local copies, waits for them, and re-layouts  8.01 us
  transfers between devices with their start and end apart: 10, of which 7 were waited for; matrix products, arithmetic and copies ran while one was open for 5% of the time, Pallas kernels for 16%

commit v1 on v0

--- a/solution.py
+++ b/solution.py
@@ -1,3 +1,5 @@
+import functools
+
 import jax
 import jax.numpy as jnp
 from jax import lax
@@ -80,7 +82,7 @@
             out_ref[g, size // 2 + h] = feats[g * GW : (g + 1) * GW, h * 128 : (h + 1) * 128]
 
 
-def weight_kernel(flag_ref, kern_ref, out_ref, base_ref):
+def weight_kernel(inner, flag_ref, kern_ref, out_ref, base_ref):
     block = pl.program_id(0)
 
     @pl.when(block == 0)
@@ -95,7 +97,7 @@
     k = lax.broadcasted_iota(jnp.int32, (1, 960), 1)
     k = k - 320 * ((k >= 320).astype(jnp.int32) + (k >= 640).astype(jnp.int32))
     for c in range(8):
-        at = block * 8 + c
+        at = (block + 5 if inner else block + 6 * (block // 5)) * 8 + c
         low, high = flag_ref[1, at].astype(jnp.float32), flag_ref[2, at].astype(jnp.float32)
         mask = jnp.where(k < 32 * c + 32, low, jnp.where(k >= 32 * c + 64, high, 1.0))
         rows = base_ref[c, pl.ds(pl.multiple_of(flag_ref[0, at] * GW, GW), GW), :]
@@ -294,22 +296,26 @@
     choose = jnp.sum(onehot * table[:, 0][None, :], axis=1)
     flags = jnp.stack([choose, sec[:-2] == middle, sec[2:] == middle]).astype(jnp.int32)
     kern = conv_bank[:, 0].transpose(0, 3, 2, 1, 4).reshape(64, 288)
-    weights = pl.pallas_call(
-        weight_kernel,
-        out_shape=jax.ShapeDtypeStruct((16, 256, 960), jnp.bfloat16),
-        grid_spec=pltpu.PrefetchScalarGridSpec(
-            num_scalar_prefetch=1,
-            grid=(16,),
-            in_specs=[whole(64, 288)],
-            out_specs=pl.BlockSpec((1, 256, 960), lambda i, s: (i, 0, 0)),
-            scratch_shapes=[pltpu.VMEM((8, 64, 960), jnp.float32)],
-        ),
-        cost_estimate=pl.CostEstimate(
-            flops=8 * 2 * 64 * 288 * 960, bytes_accessed=8 << 20, transcendentals=0
-        ),
-        name="weights",
-    )(flags, kern)
-
+
+    def weights(inner):
+        count = 6 if inner else 10
+        return pl.pallas_call(
+            functools.partial(weight_kernel, inner),
+            out_shape=jax.ShapeDtypeStruct((count, 256, 960), jnp.bfloat16),
+            grid_spec=pltpu.PrefetchScalarGridSpec(
+                num_scalar_prefetch=1,
+                grid=(count,),
+                in_specs=[whole(64, 288)],
+                out_specs=pl.BlockSpec((1, 256, 960), lambda i, s: (i, 0, 0)),
+                scratch_shapes=[pltpu.VMEM((8, 64, 960), jnp.float32)],
+            ),
+            cost_estimate=pl.CostEstimate(
+                flops=8 * 2 * 64 * 288 * 960, bytes_accessed=4 << 20, transcendentals=0
+            ),
+            name="weights",
+        )(flags, kern)
+
+    inner_weights, outer_weights = weights(True), weights(False)
     q = jnp.arange(8, dtype=jnp.int32)
     slot = (2 * ((y + TURN - (q >> 1)) & 3) + ((q & 1) ^ z2)).astype(jnp.int32)
     at = jnp.arange(21 * 128, dtype=jnp.int32)
@@ -328,7 +334,7 @@
             in_specs=[
                 whole(8, 34, GW, 128),
                 whole(128, 21 * 128),
-                pl.BlockSpec((1, 256, 960), lambda i, s: (i + 5, 0, 0)),
+                pl.BlockSpec((1, 256, 960), lambda i, s: (i, 0, 0)),
             ],
             out_specs=(
                 pl.BlockSpec((8, GW, 512), lambda i, s: (i + 5, 0, 0)),
@@ -340,7 +346,7 @@
             flops=6 * 2 * 256 * 960 * 512, bytes_accessed=8 << 20, transcendentals=0
         ),
         name="conv_inner",
-    )(slot, recv[0], spread, weights)
+    )(slot, recv[0], spread, inner_weights)
     return pl.pallas_call(
         outer_kernel,
         out_shape=jax.ShapeDtypeStruct((128, GW, 512), jnp.bfloat16),
@@ -351,7 +357,7 @@
                 whole(8, 35, GW, 128),
                 whole(128, 21 * 128),
                 whole(3, 18, GW, 512),
-                pl.BlockSpec((1, 256, 960), lambda i, s: (i + 6 * (i // 5), 0, 0)),
+                pl.BlockSpec((1, 256, 960), lambda i, s: (i, 0, 0)),
                 pl.BlockSpec(memory_space=pl.ANY),
             ],
             out_specs=pl.BlockSpec((8, GW, 512), lambda i, s: (i + 6 * (i // 5), 0, 0)),
@@ -362,7 +368,7 @@
             flops=10 * 2 * 256 * 960 * 512, bytes_accessed=8 << 20, transcendentals=0
         ),
         name="conv_outer",
-    )(slot, recv[1], spread, side, weights, part)
+    )(slot, recv[1], spread, side, outer_weights, part)
 
 
 def solution(mesh):

time: 173 us -> 173 us (level)
  Pallas kernels: 46.3 us -> 48.7 us
  waiting for transfers between devices: 67.4 us -> 65 us
    all_to_all x2, waiting for transfers between devices: 4.22 us -> 1.78 us  [shards(): recv.append(lax.all_to_all(feats, 'fiber', 0, 0, tiled=True))]
    pallas_call x1 -> x2, Pallas kernels: 9.55 us -> 12 us  [weights(): pl.pallas_call(functools.partial(weight_kernel, inner), out_shape=jax.Sha...]
  transfers between devices with their start and end apart: 10 -> 10, of which waited for: 7 -> 7; matrix products, arithmetic and copies ran while one was open for 5% -> 5% of each run, Pallas kernels for 16% -> 18%
where the time goes in v1:
time: 173 us; the launch traced here: 170 us
  waiting for transfers between devices  65 us (38%)
  Pallas kernels  48.7 us (28%)
  starting transfers between devices  41.4 us (24%)
  local copies, waits for them, and re-layouts  11 us (6%)
  other arithmetic  3.3 us (2%)
    ppermute x8, waiting for transfers between devices, send(): return lax.ppermute(part, axes, perm)  63.2 us
    ppermute x8, starting transfers between devices, send(): return lax.ppermute(part, axes, perm)  28.5 us
    pallas_call x1, Pallas kernels, shards(): pl.pallas_call(outer_kernel, out_shape=jax.ShapeDtypeStruct((128, GW, 512...  14 us
    all_to_all x2, starting transfers between devices, shards(): recv.append(lax.all_to_all(feats, 'fiber', 0, 0, tiled=True))  12.9 us
    pallas_call x1, Pallas kernels, shards(): pl.pallas_call(inner_kernel, out_shape=(jax.ShapeDtypeStruct((128, GW, 51...  12 us
    pallas_call x2, Pallas kernels, weights(): pl.pallas_call(functools.partial(weight_kernel, inner), out_shape=jax.Sha...  12 us
    pallas_call x2, Pallas kernels, shards(): pl.pallas_call(filter_kernel, out_shape=jax.ShapeDtypeStruct((8, size //...  8.91 us
    unnamed x27, local copies, waits for them, and re-layouts  7.91 us
  transfers between devices with their start and end apart: 10, of which 7 were waited for; matrix products, arithmetic and copies ran while one was open for 5% of the time, Pallas kernels for 18%

profile of v1, /device:TPU:16, one launch (start us, length us, event | category | flops | bytes accessed | tf_op | source)
XLA Modules:
  0.0 169.7 jit_solution(526262916814366686)
XLA Ops:
  0.0 0.0 copy-start
  0.0 1.7 dynamic-slice_bitcast_fusion
  1.7 0.2 copy.21
  2.0 5.6 %collective-permute-start.6 = (bf16[2,64,16,128]{3,2,1,0:T(8,128)(2,1)S(1)}, bf16[2,64,16,128]{3,2,1,0:T(8,128)(2,1)S(1)}, u32[]{:S(2)}, u32[]{:S(2)}) collective-permute-start(bf16[2,64,16,128]{3,2,1,0:T(8,128)(2,1)S(1)} %slice.73), channel_id=1, source_target_pairs={{0,16},{8,24},{1,49},{9,57},{16,17},{24,25},{17,48},{25,56},{32,1}... | collective-permute-start | bytes 1572872 | tf_op jit(solution)/shard_map/ppermute | solution.py:237
  7.6 0.2 copy.20
  7.8 5.1 %collective-permute-start.5 = (bf16[2,64,16,128]{3,2,1,0:T(8,128)(2,1)S(1)}, bf16[2,64,16,128]{3,2,1,0:T(8,128)(2,1)S(1)}, u32[]{:S(2)}, u32[]{:S(2)}) collective-permute-start(bf16[2,64,16,128]{3,2,1,0:T(8,128)(2,1)S(1)} %slice.72), channel_id=1, source_target_pairs={{0,0},{8,8},{1,33},{9,41},{16,1},{24,9},{17,32},{25,40},{32,17},{4... | collective-permute-start | bytes 1572872 | tf_op jit(solution)/shard_map/ppermute | solution.py:237
  12.9 10.5 %collective-permute-done.6.second_ref = bf16[2,64,16,128]{3,2,1,0:T(8,128)(2,1)S(1)} collective-permute-done((bf16[2,64,16,128]{3,2,1,0:T(8,128)(2,1)S(1)}, bf16[2,64,16,128]{3,2,1,0:T(8,128)(2,1)S(1)}, u32[]{:S(2)}, u32[]{:S(2)}) %collective-permute-start.6) | collective-permute-done | bytes 524320 | tf_op jit(solution)/shard_map/ppermute | solution.py:237
  23.5 10.5 %collective-permute-done.5.first_ref = bf16[2,64,16,128]{3,2,1,0:T(8,128)(2,1)S(1)} collective-permute-done((bf16[2,64,16,128]{3,2,1,0:T(8,128)(2,1)S(1)}, bf16[2,64,16,128]{3,2,1,0:T(8,128)(2,1)S(1)}, u32[]{:S(2)}, u32[]{:S(2)}) %collective-permute-start.5) | collective-permute-done | bytes 524320 | tf_op jit(solution)/shard_map/ppermute | solution.py:237
  34.0 0.1 pad_maximum_fusion.3
  34.1 0.1 collective-permute-start.7
  34.2 1.8 %flip.1.taps_ref = bf16[256,512]{1,0:T(8,128)(2,1)} custom-call(bf16[512,256]{1,0:T(8,128)(2,1)} %taps_ref.1), custom_call_target="tpu_custom_call" | custom-call | bytes 524288 | tf_op jit(solution)/shard_map/flip/pallas_call | solution.py:257
  36.0 0.6 pad_add_fusion.1.where_ref
  36.6 0.0 collective-permute-done.7.other_ref
  36.6 0.0 copy-done.5
  36.6 0.0 copy-done.6
  36.6 0.0 copy-start.7
  36.6 0.8 copy-done.7
  37.4 4.4 %filterbank.3 = bf16[8,34,32,128]{3,2,1,0:T(8,128)(2,1)} custom-call(s32[3]{0:T(128)} %pad_add_fusion.1.where_ref, bf16[2,64,16,128]{3,2,1,0:T(8,128)(2,1)} %copy-done.6, bf16[2,64,16,128]{3,2,1,0:T(8,128)(2,1)} %copy-done.5, bf16[2,64,16,128]{3,2,1,0:T(8,128)(2,1)} %copy-done.7, bf16[256,512]{1,0:T(8,128)(2,1)} %flip.1.taps_ref), custom_call_target="tpu_custom_call" | custom-call | flops 1073741824 | bytes 3145728 | tf_op jit(solution)/shard_map/filterbank/pallas_call | solution.py:271
  41.7 4.1 %all-to-all-start.1 = ((bf16[8,34,32,128]{3,2,1,0:T(8,128)(2,1)}), bf16[8,34,32,128]{3,2,1,0:T(8,128)(2,1)S(1)}, u32[]{:S(2)}, u32[]{:S(2)}) async-start(bf16[8,34,32,128]{3,2,1,0:T(8,128)(2,1)} %filterbank.3), calls=%async_computation.1 | async-start | bytes 4456448 | tf_op jit(solution)/shard_map/all_to_all | solution.py:285
  45.8 0.8 fusion.29
  46.6 1.3 collective-permute-start.1
  47.9 4.6 %collective-permute-start = (bf16[1,2048]{1,0:T(2,128)(2,1)S(1)}, bf16[1,2048]{1,0:T(2,128)(2,1)S(1)}, u32[]{:S(2)}, u32[]{:S(2)}) collective-permute-start(bf16[1,2048]{1,0:T(2,128)(2,1)S(1)} %get-tuple-element.26), channel_id=1, source_target_pairs={{0,1},{1,2},{2,3},{3,4},{4,5},{5,6},{6,7},{8,9},{9,10},{10,11},{11... | collective-permute-start | bytes 12296 | tf_op jit(solution)/shard_map/ppermute | solution.py:237
  52.5 21.4 %collective-permute-done.1 = bf16[1,2048]{1,0:T(2,128)(2,1)S(1)} collective-permute-done((bf16[1,2048]{1,0:T(2,128)(2,1)S(1)}, bf16[1,2048]{1,0:T(2,128)(2,1)S(1)}, u32[]{:S(2)}, u32[]{:S(2)}) %collective-permute-start.1) | collective-permute-done | bytes 4128 | tf_op jit(solution)/shard_map/ppermute | solution.py:237
  73.8 0.0 collective-permute-done
  73.8 0.9 fusion.28
  74.7 0.1 concatenate.12
  74.9 1.7 dynamic-slice_bitcast_fusion.2
  76.5 0.2 copy.19
  76.8 0.1 pad_maximum_fusion.1
  76.9 7.1 %collective-permute-start.3 = (bf16[2,66,16,128]{3,2,1,0:T(8,128)(2,1)S(1)}, bf16[2,66,16,128]{3,2,1,0:T(8,128)(2,1)S(1)}, u32[]{:S(2)}, u32[]{:S(2)}) collective-permute-start(bf16[2,66,16,128]{3,2,1,0:T(8,128)(2,1)S(1)} %pad_maximum_fusion.1), channel_id=1, source_target_pairs={{0,16},{8,24},{1,49},{9,57},{16,17},{24,25},{17,48},{25,56},{32,1}... | collective-permute-start | bytes 1622024 | tf_op jit(solution)/shard_map/ppermute | solution.py:237
  84.1 0.2 copy.17
  84.3 0.1 pad_maximum_fusion
  84.4 4.6 %collective-permute-start.2 = (bf16[2,66,16,128]{3,2,1,0:T(8,128)(2,1)S(1)}, bf16[2,66,16,128]{3,2,1,0:T(8,128)(2,1)S(1)}, u32[]{:S(2)}, u32[]{:S(2)}) collective-permute-start(bf16[2,66,16,128]{3,2,1,0:T(8,128)(2,1)S(1)} %pad_maximum_fusion), channel_id=1, source_target_pairs={{0,0},{8,8},{1,33},{9,41},{16,1},{24,9},{17,32},{25,40},{32,17},{4... | collective-permute-start | bytes 1622024 | tf_op jit(solution)/shard_map/ppermute | solution.py:237
  89.1 8.5 %collective-permute-done.3.second_ref = bf16[2,66,16,128]{3,2,1,0:T(8,128)(2,1)S(1)} collective-permute-done((bf16[2,66,16,128]{3,2,1,0:T(8,128)(2,1)S(1)}, bf16[2,66,16,128]{3,2,1,0:T(8,128)(2,1)S(1)}, u32[]{:S(2)}, u32[]{:S(2)}) %collective-permute-start.3) | collective-permute-done | bytes 540704 | tf_op jit(solution)/shard_map/ppermute | solution.py:237
  97.6 10.3 %collective-permute-done.2.first_ref = bf16[2,66,16,128]{3,2,1,0:T(8,128)(2,1)S(1)} collective-permute-done((bf16[2,66,16,128]{3,2,1,0:T(8,128)(2,1)S(1)}, bf16[2,66,16,128]{3,2,1,0:T(8,128)(2,1)S(1)}, u32[]{:S(2)}, u32[]{:S(2)}) %collective-permute-start.2) | collective-permute-done | bytes 540704 | tf_op jit(solution)/shard_map/ppermute | solution.py:237
  107.9 0.1 pad_maximum_fusion.2
  107.9 0.1 collective-permute-start.4
  108.0 2.1 %collective-permute-done.4.other_ref = bf16[2,66,16,128]{3,2,1,0:T(8,128)(2,1)} collective-permute-done((bf16[2,66,16,128]{3,2,1,0:T(8,128)(2,1)S(1)}, bf16[2,66,16,128]{3,2,1,0:T(8,128)(2,1)}, u32[]{:S(2)}, u32[]{:S(2)}) %collective-permute-start.4) | collective-permute-done | bytes 540704 | tf_op jit(solution)/shard_map/ppermute | solution.py:237
  110.1 0.0 copy-done.3
  110.1 0.0 copy-done.4
  110.1 4.6 %filterbank.2 = bf16[8,35,32,128]{3,2,1,0:T(8,128)(2,1)} custom-call(s32[3]{0:T(128)} %pad_add_fusion.1.where_ref, bf16[2,66,16,128]{3,2,1,0:T(8,128)(2,1)} %copy-done.4, bf16[2,66,16,128]{3,2,1,0:T(8,128)(2,1)} %copy-done.3, bf16[2,66,16,128]{3,2,1,0:T(8,128)(2,1)} %collective-permute-done.4.other_ref, bf16[256,512]{1,0:T(8,128)(2,1)} %flip.1.taps_ref), custom_call_target="tpu_custom_call" | custom-call | flops 1107296256 | bytes 3244032 | tf_op jit(solution)/shard_map/filterbank/pallas_call | solution.py:271
  114.7 0.0 all-to-all-done.1.recv_ref
  114.7 0.0 copy-start.2
  114.7 1.4 copy-done.2
  116.1 8.8 %all-to-all-start = ((bf16[8,35,32,128]{3,2,1,0:T(8,128)(2,1)}), bf16[8,35,32,128]{3,2,1,0:T(8,128)(2,1)S(1)}, u32[]{:S(2)}, u32[]{:S(2)}) async-start(bf16[8,35,32,128]{3,2,1,0:T(8,128)(2,1)} %filterbank.2), calls=%async_computation | async-start | bytes 4587520 | tf_op jit(solution)/shard_map/all_to_all | solution.py:285
  124.9 0.0 copy-done.9
  124.9 0.1 concatenate.15
  125.0 0.1 dynamic_slice.48
  125.1 0.1 slice.65
  125.2 0.0 copy-done.8
  125.2 0.1 copy.15
  125.3 0.8 reshape.77.kern_ref
  126.1 0.0 copy-done
  126.1 0.2 select_reduce_fusion
  126.2 0.1 fusion.25
  126.3 0.6 pad_add_fusion.flag_ref
  126.9 5.2 %weights.2.w_ref = bf16[6,256,960]{2,1,0:T(8,128)(2,1)} custom-call(s32[3,128]{1,0:T(4,128)} %pad_add_fusion.flag_ref, bf16[64,288]{1,0:T(8,128)(2,1)} %reshape.77.kern_ref), custom_call_target="tpu_custom_call" | custom-call | flops 283115520 | bytes 4194304 | tf_op jit(solution)/shard_map/weights/pallas_call | solution.py:302
  132.1 6.8 %weights.3.w_ref = bf16[10,256,960]{2,1,0:T(8,128)(2,1)} custom-call(s32[3,128]{1,0:T(4,128)} %pad_add_fusion.flag_ref, bf16[64,288]{1,0:T(8,128)(2,1)} %reshape.77.kern_ref), custom_call_target="tpu_custom_call" | custom-call | flops 283115520 | bytes 4194304 | tf_op jit(solution)/shard_map/weights/pallas_call | solution.py:302
  138.9 0.6 xor_add_fusion.slot_ref
  139.5 1.0 fusion.spread_ref
  140.5 12.0 %conv_inner.1 = (bf16[128,32,512]{2,1,0:T(8,128)(2,1)}, bf16[3,18,32,512]{3,2,1,0:T(8,128)(2,1)}) custom-call(s32[8]{0:T(128)} %xor_add_fusion.slot_ref, bf16[8,34,32,128]{3,2,1,0:T(8,128)(2,1)} %copy-done.2, bf16[128,2688]{1,0:T(8,128)(2,1)} %fusion.spread_ref, bf16[6,256,960]{2,1,0:T(8,128)(2,1)} %weights.2.w_ref), custom_call_target="tpu_custom_call" | custom-call | flops 1509949440 | bytes 8388608 | tf_op jit(solution)/shard_map/conv_inner/pallas_call | solution.py:325
  152.5 1.8 %all-to-all-done.recv_ref = bf16[8,35,32,128]{3,2,1,0:T(8,128)(2,1)S(1)} async-done(((bf16[8,35,32,128]{3,2,1,0:T(8,128)(2,1)}), bf16[8,35,32,128]{3,2,1,0:T(8,128)(2,1)S(1)}, u32[]{:S(2)}, u32[]{:S(2)}) %all-to-all-start) | async-done | bytes 2293792 | tf_op jit(solution)/shard_map/all_to_all | solution.py:285
  154.3 1.4 copy-done.1
  155.7 14.0 %conv_outer.1 = bf16[128,32,512]{2,1,0:T(8,128)(2,1)} custom-call(s32[8]{0:T(128)} %xor_add_fusion.slot_ref, bf16[8,35,32,128]{3,2,1,0:T(8,128)(2,1)} %copy-done.1, bf16[128,2688]{1,0:T(8,128)(2,1)} %fusion.spread_ref, bf16[3,18,32,512]{3,2,1,0:T(8,128)(2,1)} %get-tuple-element.13.side_ref, ...), custom_call_target="tpu_custom_call", output_to_operand_aliasing={{}: (5, {})} | custom-call | flops 2516582400 | bytes 8388608 | tf_op jit(solution)/shard_map/conv_outer/pallas_call | solution.py:350
  (19 shorter events, 0.3 us)
Async XLA Ops:
  0.0 126.1 %copy-start = (s32[128,8]{0,1:T(8,128)S(1)}, s32[128,8]{0,1:T(8,128)}, u32[]{:S(2)}) copy-start(s32[128,8]{0,1:T(8,128)} %param.9) | copy-start | bytes 12292
  2.0 21.5 %collective-permute-start.6 = (bf16[2,64,16,128]{3,2,1,0:T(8,128)(2,1)S(1)}, bf16[2,64,16,128]{3,2,1,0:T(8,128)(2,1)S(1)}, u32[]{:S(2)}, u32[]{:S(2)}) collective-permute-start(bf16[2,64,16,128]{3,2,1,0:T(8,128)(2,1)S(1)} %slice.73), channel_id=1, source_target_pairs={{0,16},{8,24},{1,49},{9,57},{16,17},{24,25},{17,48},{25,56},{32,1}... | collective-permute-start | bytes 1572872 | tf_op jit(solution)/shard_map/ppermute | solution.py:237
  7.8 26.1 %collective-permute-start.5 = (bf16[2,64,16,128]{3,2,1,0:T(8,128)(2,1)S(1)}, bf16[2,64,16,128]{3,2,1,0:T(8,128)(2,1)S(1)}, u32[]{:S(2)}, u32[]{:S(2)}) collective-permute-start(bf16[2,64,16,128]{3,2,1,0:T(8,128)(2,1)S(1)} %slice.72), channel_id=1, source_target_pairs={{0,0},{8,8},{1,33},{9,41},{16,1},{24,9},{17,32},{25,40},{32,17},{4... | collective-permute-start | bytes 1572872 | tf_op jit(solution)/shard_map/ppermute | solution.py:237
  23.5 13.1 %copy-start.5 = (bf16[2,64,16,128]{3,2,1,0:T(8,128)(2,1)}, bf16[2,64,16,128]{3,2,1,0:T(8,128)(2,1)S(1)}, u32[]{:S(2)}) copy-start(bf16[2,64,16,128]{3,2,1,0:T(8,128)(2,1)S(1)} %collective-permute-done.6.second_ref) | copy-start | bytes 1572868
  34.0 2.6 %copy-start.6 = (bf16[2,64,16,128]{3,2,1,0:T(8,128)(2,1)}, bf16[2,64,16,128]{3,2,1,0:T(8,128)(2,1)S(1)}, u32[]{:S(2)}) copy-start(bf16[2,64,16,128]{3,2,1,0:T(8,128)(2,1)S(1)} %collective-permute-done.5.first_ref) | copy-start | bytes 1572868
  34.1 2.5 %collective-permute-start.7 = (bf16[2,64,16,128]{3,2,1,0:T(8,128)(2,1)S(1)}, bf16[2,64,16,128]{3,2,1,0:T(8,128)(2,1)S(1)}, u32[]{:S(2)}, u32[]{:S(2)}) collective-permute-start(bf16[2,64,16,128]{3,2,1,0:T(8,128)(2,1)S(1)} %pad_maximum_fusion.3), channel_id=1, source_target_pairs={{0,8},{8,0},{16,24},{24,16},{32,40},{40,32},{48,56},{56,48},{64,72... | collective-permute-start | bytes 1572872 | tf_op jit(solution)/shard_map/ppermute | solution.py:237
  36.6 0.8 copy-start.7
  41.7 72.9 %all-to-all-start.1 = ((bf16[8,34,32,128]{3,2,1,0:T(8,128)(2,1)}), bf16[8,34,32,128]{3,2,1,0:T(8,128)(2,1)S(1)}, u32[]{:S(2)}, u32[]{:S(2)}) async-start(bf16[8,34,32,128]{3,2,1,0:T(8,128)(2,1)} %filterbank.3), calls=%async_computation.1 | async-start | bytes 4456448 | tf_op jit(solution)/shard_map/all_to_all | solution.py:285
  46.6 27.3 %collective-permute-start.1 = (bf16[1,2048]{1,0:T(2,128)(2,1)S(1)}, bf16[1,2048]{1,0:T(2,128)(2,1)S(1)}, u32[]{:S(2)}, u32[]{:S(2)}) collective-permute-start(bf16[1,2048]{1,0:T(2,128)(2,1)S(1)} %get-tuple-element.25), channel_id=1, source_target_pairs={{1,0},{2,1},{3,2},{4,3},{5,4},{6,5},{7,6},{9,8},{10,9},{11,10},{12... | collective-permute-start | bytes 12296 | tf_op jit(solution)/shard_map/ppermute | solution.py:237
  47.9 26.0 %collective-permute-start = (bf16[1,2048]{1,0:T(2,128)(2,1)S(1)}, bf16[1,2048]{1,0:T(2,128)(2,1)S(1)}, u32[]{:S(2)}, u32[]{:S(2)}) collective-permute-start(bf16[1,2048]{1,0:T(2,128)(2,1)S(1)} %get-tuple-element.26), channel_id=1, source_target_pairs={{0,1},{1,2},{2,3},{3,4},{4,5},{5,6},{6,7},{8,9},{9,10},{10,11},{11... | collective-permute-start | bytes 12296 | tf_op jit(solution)/shard_map/ppermute | solution.py:237
  76.9 20.6 %collective-permute-start.3 = (bf16[2,66,16,128]{3,2,1,0:T(8,128)(2,1)S(1)}, bf16[2,66,16,128]{3,2,1,0:T(8,128)(2,1)S(1)}, u32[]{:S(2)}, u32[]{:S(2)}) collective-permute-start(bf16[2,66,16,128]{3,2,1,0:T(8,128)(2,1)S(1)} %pad_maximum_fusion.1), channel_id=1, source_target_pairs={{0,16},{8,24},{1,49},{9,57},{16,17},{24,25},{17,48},{25,56},{32,1}... | collective-permute-start | bytes 1622024 | tf_op jit(solution)/shard_map/ppermute | solution.py:237
  84.4 23.4 %collective-permute-start.2 = (bf16[2,66,16,128]{3,2,1,0:T(8,128)(2,1)S(1)}, bf16[2,66,16,128]{3,2,1,0:T(8,128)(2,1)S(1)}, u32[]{:S(2)}, u32[]{:S(2)}) collective-permute-start(bf16[2,66,16,128]{3,2,1,0:T(8,128)(2,1)S(1)} %pad_maximum_fusion), channel_id=1, source_target_pairs={{0,0},{8,8},{1,33},{9,41},{16,1},{24,9},{17,32},{25,40},{32,17},{4... | collective-permute-start | bytes 1622024 | tf_op jit(solution)/shard_map/ppermute | solution.py:237
  97.6 12.5 %copy-start.3 = (bf16[2,66,16,128]{3,2,1,0:T(8,128)(2,1)}, bf16[2,66,16,128]{3,2,1,0:T(8,128)(2,1)S(1)}, u32[]{:S(2)}) copy-start(bf16[2,66,16,128]{3,2,1,0:T(8,128)(2,1)S(1)} %collective-permute-done.3.second_ref) | copy-start | bytes 1622020
  107.9 2.2 %copy-start.4 = (bf16[2,66,16,128]{3,2,1,0:T(8,128)(2,1)}, bf16[2,66,16,128]{3,2,1,0:T(8,128)(2,1)S(1)}, u32[]{:S(2)}) copy-start(bf16[2,66,16,128]{3,2,1,0:T(8,128)(2,1)S(1)} %collective-permute-done.2.first_ref) | copy-start | bytes 1622020
  107.9 2.2 %collective-permute-start.4 = (bf16[2,66,16,128]{3,2,1,0:T(8,128)(2,1)S(1)}, bf16[2,66,16,128]{3,2,1,0:T(8,128)(2,1)}, u32[]{:S(2)}, u32[]{:S(2)}) collective-permute-start(bf16[2,66,16,128]{3,2,1,0:T(8,128)(2,1)S(1)} %pad_maximum_fusion.2), channel_id=1, source_target_pairs={{0,8},{8,0},{16,24},{24,16},{32,40},{40,32},{48,56},{56,48},{64,72... | collective-permute-start | bytes 1622024 | tf_op jit(solution)/shard_map/ppermute | solution.py:237
  114.7 10.3 %copy-start.9 = (s32[4096]{0:T(1024)S(1)}, s32[4096]{0:T(1024)}, u32[]{:S(2)}) copy-start(s32[4096]{0:T(1024)} %param.8) | copy-start | bytes 49156
  114.7 10.5 %copy-start.8 = (bf16[2,1,3,3,32,32]{5,4,3,2,1,0:T(8,128)(2,1)S(1)}, bf16[2,1,3,3,32,32]{5,4,3,2,1,0:T(8,128)(2,1)}, u32[]{:S(2)}) copy-start(bf16[2,1,3,3,32,32]{5,4,3,2,1,0:T(8,128)(2,1)} %param.10) | copy-start | bytes 110596
  114.7 1.5 copy-start.2
  116.1 38.2 %all-to-all-start = ((bf16[8,35,32,128]{3,2,1,0:T(8,128)(2,1)}), bf16[8,35,32,128]{3,2,1,0:T(8,128)(2,1)S(1)}, u32[]{:S(2)}, u32[]{:S(2)}) async-start(bf16[8,35,32,128]{3,2,1,0:T(8,128)(2,1)} %filterbank.2), calls=%async_computation | async-start | bytes 4587520 | tf_op jit(solution)/shard_map/all_to_all | solution.py:285
  154.3 1.4 copy-start.1

commit v2 on v0

--- a/solution.py
+++ b/solution.py
@@ -8,7 +8,7 @@
 HOP = 128
 GW = 32
 AXES = ("tm", "fiber")
-TURN = 0
+TURN = (0, 2)
 
 
 PLACES = [(x, y, z, c) for x in range(4) for y in range(4) for z in range(8) for c in range(2)]
@@ -18,16 +18,16 @@
     return ((y * 4 + z // 2) * 2 + c) * 8 + x * 2 + z % 2
 
 
-def spot(x, y, late, odd, b, core, early):
-    return flat((x - y + TURN - early) % 4, x, 4 * odd + 2 * b + (late ^ odd), core)
-
-
-def bulk_route(step):
+def spot(x, y, late, odd, b, core, early, turn):
+    return flat((x - y + turn - early) % 4, x, 4 * odd + 2 * b + (late ^ odd), core)
+
+
+def bulk_route(step, turn):
     pairs = []
     for x, y, z, c in PLACES:
         pair, odd = z // 2, z % 2
         late = 0 if pair in (0, 3) else 1
-        there = spot(x, y, late, odd, step ^ (pair // 2), c, int(pair == 3))
+        there = spot(x, y, late, odd, step ^ (pair // 2), c, int(pair == 3), turn)
         pairs.append((flat(x, y, z, c), there))
     return pairs
 
@@ -238,7 +238,7 @@
     for step in (0, 1):
         rows = lax.dynamic_slice_in_dim(waveform, 256 * (step ^ z2), 256, 0)
         part = rows.reshape(2, 128, 16, HOP)[:, 32:96]
-        got[0].append(send(part, bulk_route(step)))
+        got[0].append(send(part, bulk_route(step, TURN[0])))
     up = [(i, i + 1) for i in range(7)]
     row_low = send(waveform[511:], up, "fiber")
     row_high = send(waveform[:1], [(j, i) for i, j in up], "fiber")
@@ -250,7 +250,7 @@
         rows = rows.reshape(2, 128, 16, HOP)
         extra = lax.dynamic_slice_in_dim(sides, 2 * (step ^ z2), 2, 0)
         part = jnp.concatenate([rows[:, :32], rows[:, 96:], extra], axis=1)
-        got[1].append(send(part, bulk_route(step)))
+        got[1].append(send(part, bulk_route(step, TURN[1])))
 
     taps = pl.pallas_call(
         flip_kernel,
@@ -259,11 +259,11 @@
         name="flip",
     )(filters)
 
-    keep = jnp.where((late == 0) & (((y - x + TURN) & 3) == 0), 0, 1)
-    where = jnp.stack([first, core, keep]).astype(jnp.int32)
     recv = []
     for half in (0, 1):
         size = 66 if half else 64
+        keep = jnp.where((late == 0) & (((y - x + TURN[half]) & 3) == 0), 0, 1)
+        where = jnp.stack([first, core, keep]).astype(jnp.int32)
         theirs = [lax.dynamic_index_in_dim(g, 1 - core, 0, False) for g in got[half]]
         other = send(jnp.stack(theirs), OTHER_CORE, "tm")
         feats = pl.pallas_call(
@@ -311,7 +311,9 @@
     )(flags, kern)
 
     q = jnp.arange(8, dtype=jnp.int32)
-    slot = (2 * ((y + TURN - (q >> 1)) & 3) + ((q & 1) ^ z2)).astype(jnp.int32)
+    slot = [
+        (2 * ((y + turn - (q >> 1)) & 3) + ((q & 1) ^ z2)).astype(jnp.int32) for turn in TURN
+    ]
     at = jnp.arange(21 * 128, dtype=jnp.int32)
     source = jnp.where(at % 64 >= 61, (at % 128) // 64 * 64 + 3 * (at // 128) + at % 64 - 61, -1)
     spread = (jnp.arange(128, dtype=jnp.int32)[:, None] == source[None, :]).astype(jnp.bfloat16)
@@ -340,7 +342,7 @@
             flops=6 * 2 * 256 * 960 * 512, bytes_accessed=8 << 20, transcendentals=0
         ),
         name="conv_inner",
-    )(slot, recv[0], spread, weights)
+    )(slot[0], recv[0], spread, weights)
     return pl.pallas_call(
         outer_kernel,
         out_shape=jax.ShapeDtypeStruct((128, GW, 512), jnp.bfloat16),
@@ -362,7 +364,7 @@
             flops=10 * 2 * 256 * 960 * 512, bytes_accessed=8 << 20, transcendentals=0
         ),
         name="conv_outer",
-    )(slot, recv[1], spread, side, weights, part)
+    )(slot[1], recv[1], spread, side, weights, part)
 
 
 def solution(mesh):

time: 173 us -> 173 us (level)
  the two profiles are of different devices: /device:TPU:16 before, /device:TPU:1 now
where the time goes in v2:
time: 173 us; the launch traced here: 172 us
  waiting for transfers between devices  61.4 us (35%)
  starting transfers between devices  48.1 us (28%)
  Pallas kernels  46.3 us (27%)
  local copies, waits for them, and re-layouts  11.1 us (6%)
  other arithmetic  5.31 us (3%)
    ppermute x8, waiting for transfers between devices, send(): return lax.ppermute(part, axes, perm)  58.5 us
    all_to_all x2, starting transfers between devices, shards(): recv.append(lax.all_to_all(feats, 'fiber', 0, 0, tiled=True))  26.2 us
    ppermute x8, starting transfers between devices, send(): return lax.ppermute(part, axes, perm)  21.9 us
    pallas_call x1, Pallas kernels, shards(): pl.pallas_call(outer_kernel, out_shape=jax.ShapeDtypeStruct((128, GW, 512...  14 us
    pallas_call x1, Pallas kernels, shards(): pl.pallas_call(inner_kernel, out_shape=(jax.ShapeDtypeStruct((128, GW, 51...  12 us
    pallas_call x1, Pallas kernels, shards(): pl.pallas_call(weight_kernel, out_shape=jax.ShapeDtypeStruct((16, 256, 96...  9.55 us
    pallas_call x2, Pallas kernels, shards(): pl.pallas_call(filter_kernel, out_shape=jax.ShapeDtypeStruct((8, size //...  8.92 us
    unnamed x27, local copies, waits for them, and re-layouts  8.01 us
  transfers between devices with their start and end apart: 10, of which 6 were waited for; matrix products, arithmetic and copies ran while one was open for 6% of the time, Pallas kernels for 16%

profile of v2, /device:TPU:1, one launch (start us, length us, event | category | flops | bytes accessed | tf_op | source)
XLA Modules:
  0.0 172.5 jit_solution(5741933727572167815)
XLA Ops:
  0.0 0.0 copy-start
  0.0 1.7 dynamic-slice_bitcast_fusion
  1.7 0.2 copy.19
  2.0 3.9 %collective-permute-start.6 = (bf16[2,64,16,128]{3,2,1,0:T(8,128)(2,1)S(1)}, bf16[2,64,16,128]{3,2,1,0:T(8,128)(2,1)S(1)}, u32[]{:S(2)}, u32[]{:S(2)}) collective-permute-start(bf16[2,64,16,128]{3,2,1,0:T(8,128)(2,1)S(1)} %slice.73), channel_id=1, source_target_pairs={{0,16},{8,24},{1,49},{9,57},{16,17},{24,25},{17,48},{25,56},{32,1}... | collective-permute-start | bytes 1572872 | tf_op jit(solution)/shard_map/ppermute | solution.py:235
  5.9 0.2 copy.18
  6.1 0.7 collective-permute-start.5
  6.8 16.1 %collective-permute-done.6.second_ref = bf16[2,64,16,128]{3,2,1,0:T(8,128)(2,1)S(1)} collective-permute-done((bf16[2,64,16,128]{3,2,1,0:T(8,128)(2,1)S(1)}, bf16[2,64,16,128]{3,2,1,0:T(8,128)(2,1)S(1)}, u32[]{:S(2)}, u32[]{:S(2)}) %collective-permute-start.6) | collective-permute-done | bytes 524320 | tf_op jit(solution)/shard_map/ppermute | solution.py:235
  23.0 0.0 collective-permute-done.5.first_ref
  23.0 0.0 copy-start.6
  23.0 0.1 pad_maximum_fusion.3
  23.1 2.2 %collective-permute-start.7 = (bf16[2,64,16,128]{3,2,1,0:T(8,128)(2,1)S(1)}, bf16[2,64,16,128]{3,2,1,0:T(8,128)(2,1)S(1)}, u32[]{:S(2)}, u32[]{:S(2)}) collective-permute-start(bf16[2,64,16,128]{3,2,1,0:T(8,128)(2,1)S(1)} %pad_maximum_fusion.3), channel_id=1, source_target_pairs={{0,8},{8,0},{16,24},{24,16},{32,40},{40,32},{48,56},{56,48},{64,72... | collective-permute-start | bytes 1572872 | tf_op jit(solution)/shard_map/ppermute | solution.py:235
  25.3 1.8 %flip.1.taps_ref = bf16[256,512]{1,0:T(8,128)(2,1)} custom-call(bf16[512,256]{1,0:T(8,128)(2,1)} %taps_ref.1), custom_call_target="tpu_custom_call" | custom-call | bytes 524288 | tf_op jit(solution)/shard_map/flip/pallas_call | solution.py:255
  27.1 0.6 pad_add_fusion.3.where_ref
  27.6 0.0 collective-permute-done.7.other_ref
  27.6 0.0 copy-done.5
  27.6 0.0 copy-done.6
  27.6 0.0 copy-start.7
  27.7 0.8 copy-done.7
  28.4 4.4 %filterbank.3 = bf16[8,34,32,128]{3,2,1,0:T(8,128)(2,1)} custom-call(s32[3]{0:T(128)} %pad_add_fusion.3.where_ref, bf16[2,64,16,128]{3,2,1,0:T(8,128)(2,1)} %copy-done.6, bf16[2,64,16,128]{3,2,1,0:T(8,128)(2,1)} %copy-done.5, bf16[2,64,16,128]{3,2,1,0:T(8,128)(2,1)} %copy-done.7, bf16[256,512]{1,0:T(8,128)(2,1)} %flip.1.taps_ref), custom_call_target="tpu_custom_call" | custom-call | flops 1073741824 | bytes 3145728 | tf_op jit(solution)/shard_map/filterbank/pallas_call | solution.py:269
  32.8 16.5 %all-to-all-start.1 = ((bf16[8,34,32,128]{3,2,1,0:T(8,128)(2,1)}), bf16[8,34,32,128]{3,2,1,0:T(8,128)(2,1)S(1)}, u32[]{:S(2)}, u32[]{:S(2)}) async-start(bf16[8,34,32,128]{3,2,1,0:T(8,128)(2,1)} %filterbank.3), calls=%async_computation.1 | async-start | bytes 4456448 | tf_op jit(solution)/shard_map/all_to_all | solution.py:283
  49.3 0.8 fusion.29
  50.1 1.3 collective-permute-start.1
  51.4 4.0 %collective-permute-start = (bf16[1,2048]{1,0:T(2,128)(2,1)S(1)}, bf16[1,2048]{1,0:T(2,128)(2,1)S(1)}, u32[]{:S(2)}, u32[]{:S(2)}) collective-permute-start(bf16[1,2048]{1,0:T(2,128)(2,1)S(1)} %get-tuple-element.26), channel_id=1, source_target_pairs={{0,1},{1,2},{2,3},{3,4},{4,5},{5,6},{6,7},{8,9},{9,10},{10,11},{11... | collective-permute-start | bytes 12296 | tf_op jit(solution)/shard_map/ppermute | solution.py:235
  55.4 21.0 %collective-permute-done.1 = bf16[1,2048]{1,0:T(2,128)(2,1)S(1)} collective-permute-done((bf16[1,2048]{1,0:T(2,128)(2,1)S(1)}, bf16[1,2048]{1,0:T(2,128)(2,1)S(1)}, u32[]{:S(2)}, u32[]{:S(2)}) %collective-permute-start.1) | collective-permute-done | bytes 4128 | tf_op jit(solution)/shard_map/ppermute | solution.py:235
  76.4 0.0 collective-permute-done
  76.4 0.9 fusion.28
  77.3 0.1 concatenate.12
  77.4 1.7 dynamic-slice_bitcast_fusion.2
  79.1 0.2 copy.17
  79.4 0.1 pad_maximum_fusion.1
  79.5 4.7 %collective-permute-start.3 = (bf16[2,66,16,128]{3,2,1,0:T(8,128)(2,1)S(1)}, bf16[2,66,16,128]{3,2,1,0:T(8,128)(2,1)S(1)}, u32[]{:S(2)}, u32[]{:S(2)}) collective-permute-start(bf16[2,66,16,128]{3,2,1,0:T(8,128)(2,1)S(1)} %pad_maximum_fusion.1), channel_id=1, source_target_pairs={{0,20},{8,28},{1,53},{9,61},{16,21},{24,29},{17,52},{25,60},{32,5}... | collective-permute-start | bytes 1622024 | tf_op jit(solution)/shard_map/ppermute | solution.py:235
  84.2 0.2 copy.15
  84.5 0.1 pad_maximum_fusion
  84.5 4.7 %collective-permute-start.2 = (bf16[2,66,16,128]{3,2,1,0:T(8,128)(2,1)S(1)}, bf16[2,66,16,128]{3,2,1,0:T(8,128)(2,1)S(1)}, u32[]{:S(2)}, u32[]{:S(2)}) collective-permute-start(bf16[2,66,16,128]{3,2,1,0:T(8,128)(2,1)S(1)} %pad_maximum_fusion), channel_id=1, source_target_pairs={{0,4},{8,12},{1,37},{9,45},{16,5},{24,13},{17,36},{25,44},{32,21},... | collective-permute-start | bytes 1622024 | tf_op jit(solution)/shard_map/ppermute | solution.py:235
  89.2 7.9 %collective-permute-done.3.second_ref = bf16[2,66,16,128]{3,2,1,0:T(8,128)(2,1)S(1)} collective-permute-done((bf16[2,66,16,128]{3,2,1,0:T(8,128)(2,1)S(1)}, bf16[2,66,16,128]{3,2,1,0:T(8,128)(2,1)S(1)}, u32[]{:S(2)}, u32[]{:S(2)}) %collective-permute-start.3) | collective-permute-done | bytes 540704 | tf_op jit(solution)/shard_map/ppermute | solution.py:235
  97.1 12.2 %collective-permute-done.2.first_ref = bf16[2,66,16,128]{3,2,1,0:T(8,128)(2,1)S(1)} collective-permute-done((bf16[2,66,16,128]{3,2,1,0:T(8,128)(2,1)S(1)}, bf16[2,66,16,128]{3,2,1,0:T(8,128)(2,1)S(1)}, u32[]{:S(2)}, u32[]{:S(2)}) %collective-permute-start.2) | collective-permute-done | bytes 540704 | tf_op jit(solution)/shard_map/ppermute | solution.py:235
  109.3 0.9 pad_maximum_fusion.2
  110.3 0.5 collective-permute-start.4
  110.8 0.6 pad_add_fusion.1.where_ref
  111.4 1.3 collective-permute-done.4.other_ref
  112.7 0.0 copy-done.3
  112.7 4.5 %filterbank.2 = bf16[8,35,32,128]{3,2,1,0:T(8,128)(2,1)} custom-call(s32[3]{0:T(128)} %pad_add_fusion.1.where_ref, bf16[2,66,16,128]{3,2,1,0:T(8,128)(2,1)} %copy-done.4, bf16[2,66,16,128]{3,2,1,0:T(8,128)(2,1)} %copy-done.3, bf16[2,66,16,128]{3,2,1,0:T(8,128)(2,1)} %collective-permute-done.4.other_ref, bf16[256,512]{1,0:T(8,128)(2,1)} %flip.1.taps_ref), custom_call_target="tpu_custom_call" | custom-call | flops 1107296256 | bytes 3244032 | tf_op jit(solution)/shard_map/filterbank/pallas_call | solution.py:269
  117.2 0.0 all-to-all-done.1.recv_ref
  117.3 0.0 copy-start.2
  117.3 1.4 copy-done.2
  118.7 9.7 %all-to-all-start = ((bf16[8,35,32,128]{3,2,1,0:T(8,128)(2,1)}), bf16[8,35,32,128]{3,2,1,0:T(8,128)(2,1)S(1)}, u32[]{:S(2)}, u32[]{:S(2)}) async-start(bf16[8,35,32,128]{3,2,1,0:T(8,128)(2,1)} %filterbank.2), calls=%async_computation | async-start | bytes 4587520 | tf_op jit(solution)/shard_map/all_to_all | solution.py:283
  128.4 0.0 copy-done.9
  128.4 0.1 concatenate.15
  128.5 0.1 dynamic_slice.48
  128.6 0.1 slice.65
  128.7 0.0 copy-done.8
  128.7 0.1 copy.13
  128.8 0.8 reshape.77.kern_ref
  129.6 0.2 select_reduce_fusion
  129.8 0.1 fusion.25
  129.8 0.6 pad_add_fusion.flag_ref
  130.4 9.6 %weights.1.w_ref = bf16[16,256,960]{2,1,0:T(8,128)(2,1)} custom-call(s32[3,128]{1,0:T(4,128)} %pad_add_fusion.flag_ref, bf16[64,288]{1,0:T(8,128)(2,1)} %reshape.77.kern_ref), custom_call_target="tpu_custom_call" | custom-call | flops 283115520 | bytes 8388608 | tf_op jit(solution)/shard_map/weights/pallas_call | solution.py:297
  140.0 0.5 multiply_add_fusion.slot_ref
  140.5 0.6 multiply_add_fusion.1.slot_ref
  141.1 1.0 fusion.spread_ref
  142.1 12.0 %conv_inner.1 = (bf16[128,32,512]{2,1,0:T(8,128)(2,1)}, bf16[3,18,32,512]{3,2,1,0:T(8,128)(2,1)}) custom-call(s32[8]{0:T(128)} %multiply_add_fusion.slot_ref, bf16[8,34,32,128]{3,2,1,0:T(8,128)(2,1)} %copy-done.2, bf16[128,2688]{1,0:T(8,128)(2,1)} %fusion.spread_ref, bf16[16,256,960]{2,1,0:T(8,128)(2,1)} %weights.1.w_ref), custom_call_target="tpu_custom_call" | custom-call | flops 1509949440 | bytes 8388608 | tf_op jit(solution)/shard_map/conv_inner/pallas_call | solution.py:321
  154.1 2.8 %all-to-all-done.recv_ref = bf16[8,35,32,128]{3,2,1,0:T(8,128)(2,1)S(1)} async-done(((bf16[8,35,32,128]{3,2,1,0:T(8,128)(2,1)}), bf16[8,35,32,128]{3,2,1,0:T(8,128)(2,1)S(1)}, u32[]{:S(2)}, u32[]{:S(2)}) %all-to-all-start) | async-done | bytes 2293792 | tf_op jit(solution)/shard_map/all_to_all | solution.py:283
  157.0 1.5 copy-done.1
  158.4 14.0 %conv_outer.1 = bf16[128,32,512]{2,1,0:T(8,128)(2,1)} custom-call(s32[8]{0:T(128)} %multiply_add_fusion.1.slot_ref, bf16[8,35,32,128]{3,2,1,0:T(8,128)(2,1)} %copy-done.1, bf16[128,2688]{1,0:T(8,128)(2,1)} %fusion.spread_ref, bf16[3,18,32,512]{3,2,1,0:T(8,128)(2,1)} %get-tuple-element.13.side_ref, ...), custom_call_target="tpu_custom_call", output_to_operand_aliasing={{}: (5, {})} | custom-call | flops 2516582400 | bytes 8388608 | tf_op jit(solution)/shard_map/conv_outer/pallas_call | solution.py:346
  (20 shorter events, 0.3 us)
Async XLA Ops:
  0.0 129.6 %copy-start = (s32[128,8]{0,1:T(8,128)S(1)}, s32[128,8]{0,1:T(8,128)}, u32[]{:S(2)}) copy-start(s32[128,8]{0,1:T(8,128)} %param.9) | copy-start | bytes 12292
  2.0 21.0 %collective-permute-start.6 = (bf16[2,64,16,128]{3,2,1,0:T(8,128)(2,1)S(1)}, bf16[2,64,16,128]{3,2,1,0:T(8,128)(2,1)S(1)}, u32[]{:S(2)}, u32[]{:S(2)}) collective-permute-start(bf16[2,64,16,128]{3,2,1,0:T(8,128)(2,1)S(1)} %slice.73), channel_id=1, source_target_pairs={{0,16},{8,24},{1,49},{9,57},{16,17},{24,25},{17,48},{25,56},{32,1}... | collective-permute-start | bytes 1572872 | tf_op jit(solution)/shard_map/ppermute | solution.py:235
  6.1 16.9 %collective-permute-start.5 = (bf16[2,64,16,128]{3,2,1,0:T(8,128)(2,1)S(1)}, bf16[2,64,16,128]{3,2,1,0:T(8,128)(2,1)S(1)}, u32[]{:S(2)}, u32[]{:S(2)}) collective-permute-start(bf16[2,64,16,128]{3,2,1,0:T(8,128)(2,1)S(1)} %slice.72), channel_id=1, source_target_pairs={{0,0},{8,8},{1,33},{9,41},{16,1},{24,9},{17,32},{25,40},{32,17},{4... | collective-permute-start | bytes 1572872 | tf_op jit(solution)/shard_map/ppermute | solution.py:235
  23.0 4.7 %copy-start.5 = (bf16[2,64,16,128]{3,2,1,0:T(8,128)(2,1)}, bf16[2,64,16,128]{3,2,1,0:T(8,128)(2,1)S(1)}, u32[]{:S(2)}) copy-start(bf16[2,64,16,128]{3,2,1,0:T(8,128)(2,1)S(1)} %collective-permute-done.6.second_ref) | copy-start | bytes 1572868
  23.0 4.6 %copy-start.6 = (bf16[2,64,16,128]{3,2,1,0:T(8,128)(2,1)}, bf16[2,64,16,128]{3,2,1,0:T(8,128)(2,1)S(1)}, u32[]{:S(2)}) copy-start(bf16[2,64,16,128]{3,2,1,0:T(8,128)(2,1)S(1)} %collective-permute-done.5.first_ref) | copy-start | bytes 1572868
  23.1 4.5 %collective-permute-start.7 = (bf16[2,64,16,128]{3,2,1,0:T(8,128)(2,1)S(1)}, bf16[2,64,16,128]{3,2,1,0:T(8,128)(2,1)S(1)}, u32[]{:S(2)}, u32[]{:S(2)}) collective-permute-start(bf16[2,64,16,128]{3,2,1,0:T(8,128)(2,1)S(1)} %pad_maximum_fusion.3), channel_id=1, source_target_pairs={{0,8},{8,0},{16,24},{24,16},{32,40},{40,32},{48,56},{56,48},{64,72... | collective-permute-start | bytes 1572872 | tf_op jit(solution)/shard_map/ppermute | solution.py:235
  27.6 0.8 copy-start.7
  32.8 84.4 %all-to-all-start.1 = ((bf16[8,34,32,128]{3,2,1,0:T(8,128)(2,1)}), bf16[8,34,32,128]{3,2,1,0:T(8,128)(2,1)S(1)}, u32[]{:S(2)}, u32[]{:S(2)}) async-start(bf16[8,34,32,128]{3,2,1,0:T(8,128)(2,1)} %filterbank.3), calls=%async_computation.1 | async-start | bytes 4456448 | tf_op jit(solution)/shard_map/all_to_all | solution.py:283
  50.1 26.3 %collective-permute-start.1 = (bf16[1,2048]{1,0:T(2,128)(2,1)S(1)}, bf16[1,2048]{1,0:T(2,128)(2,1)S(1)}, u32[]{:S(2)}, u32[]{:S(2)}) collective-permute-start(bf16[1,2048]{1,0:T(2,128)(2,1)S(1)} %get-tuple-element.25), channel_id=1, source_target_pairs={{1,0},{2,1},{3,2},{4,3},{5,4},{6,5},{7,6},{9,8},{10,9},{11,10},{12... | collective-permute-start | bytes 12296 | tf_op jit(solution)/shard_map/ppermute | solution.py:235
  51.4 25.0 %collective-permute-start = (bf16[1,2048]{1,0:T(2,128)(2,1)S(1)}, bf16[1,2048]{1,0:T(2,128)(2,1)S(1)}, u32[]{:S(2)}, u32[]{:S(2)}) collective-permute-start(bf16[1,2048]{1,0:T(2,128)(2,1)S(1)} %get-tuple-element.26), channel_id=1, source_target_pairs={{0,1},{1,2},{2,3},{3,4},{4,5},{5,6},{6,7},{8,9},{9,10},{10,11},{11... | collective-permute-start | bytes 12296 | tf_op jit(solution)/shard_map/ppermute | solution.py:235
  79.5 17.6 %collective-permute-start.3 = (bf16[2,66,16,128]{3,2,1,0:T(8,128)(2,1)S(1)}, bf16[2,66,16,128]{3,2,1,0:T(8,128)(2,1)S(1)}, u32[]{:S(2)}, u32[]{:S(2)}) collective-permute-start(bf16[2,66,16,128]{3,2,1,0:T(8,128)(2,1)S(1)} %pad_maximum_fusion.1), channel_id=1, source_target_pairs={{0,20},{8,28},{1,53},{9,61},{16,21},{24,29},{17,52},{25,60},{32,5}... | collective-permute-start | bytes 1622024 | tf_op jit(solution)/shard_map/ppermute | solution.py:235
  84.5 24.8 %collective-permute-start.2 = (bf16[2,66,16,128]{3,2,1,0:T(8,128)(2,1)S(1)}, bf16[2,66,16,128]{3,2,1,0:T(8,128)(2,1)S(1)}, u32[]{:S(2)}, u32[]{:S(2)}) collective-permute-start(bf16[2,66,16,128]{3,2,1,0:T(8,128)(2,1)S(1)} %pad_maximum_fusion), channel_id=1, source_target_pairs={{0,4},{8,12},{1,37},{9,45},{16,5},{24,13},{17,36},{25,44},{32,21},... | collective-permute-start | bytes 1622024 | tf_op jit(solution)/shard_map/ppermute | solution.py:235
  97.1 15.6 %copy-start.3 = (bf16[2,66,16,128]{3,2,1,0:T(8,128)(2,1)}, bf16[2,66,16,128]{3,2,1,0:T(8,128)(2,1)S(1)}, u32[]{:S(2)}) copy-start(bf16[2,66,16,128]{3,2,1,0:T(8,128)(2,1)S(1)} %collective-permute-done.3.second_ref) | copy-start | bytes 1622020
  109.3 3.4 %copy-start.4 = (bf16[2,66,16,128]{3,2,1,0:T(8,128)(2,1)}, bf16[2,66,16,128]{3,2,1,0:T(8,128)(2,1)S(1)}, u32[]{:S(2)}) copy-start(bf16[2,66,16,128]{3,2,1,0:T(8,128)(2,1)S(1)} %collective-permute-done.2.first_ref) | copy-start | bytes 1622020
  110.3 2.4 %collective-permute-start.4 = (bf16[2,66,16,128]{3,2,1,0:T(8,128)(2,1)}, bf16[2,66,16,128]{3,2,1,0:T(8,128)(2,1)}, u32[]{:S(2)}, u32[]{:S(2)}) collective-permute-start(bf16[2,66,16,128]{3,2,1,0:T(8,128)(2,1)} %pad_maximum_fusion.2), channel_id=1, source_target_pairs={{0,8},{8,0},{16,24},{24,16},{32,40},{40,32},{48,56},{56,48},{64,72... | collective-permute-start | bytes 1622024 | tf_op jit(solution)/shard_map/ppermute | solution.py:235
  117.2 11.2 %copy-start.9 = (s32[4096]{0:T(1024)S(1)}, s32[4096]{0:T(1024)}, u32[]{:S(2)}) copy-start(s32[4096]{0:T(1024)} %param.8) | copy-start | bytes 49156
  117.2 11.4 %copy-start.8 = (bf16[2,1,3,3,32,32]{5,4,3,2,1,0:T(8,128)(2,1)S(1)}, bf16[2,1,3,3,32,32]{5,4,3,2,1,0:T(8,128)(2,1)}, u32[]{:S(2)}) copy-start(bf16[2,1,3,3,32,32]{5,4,3,2,1,0:T(8,128)(2,1)} %param.10) | copy-start | bytes 110596
  117.3 1.5 copy-start.2
  118.7 38.3 %all-to-all-start = ((bf16[8,35,32,128]{3,2,1,0:T(8,128)(2,1)}), bf16[8,35,32,128]{3,2,1,0:T(8,128)(2,1)S(1)}, u32[]{:S(2)}, u32[]{:S(2)}) async-start(bf16[8,35,32,128]{3,2,1,0:T(8,128)(2,1)} %filterbank.2), calls=%async_computation | async-start | bytes 4587520 | tf_op jit(solution)/shard_map/all_to_all | solution.py:283
  157.0 1.5 copy-start.1

commit v3 on v0

--- a/solution.py
+++ b/solution.py
@@ -158,9 +158,9 @@
 
     @pl.when(step == 0)
     def _():
-        place_early(late_ref, lambda q, h: recv_ref[slot_ref[q], 32 + h], spread_ref)
-
-        @pl.loop(0, 8)
+        place_early(late_ref, lambda q, h: recv_ref[slot_ref[q], 24 + h], spread_ref)
+
+        @pl.loop(0, 6)
         def _(g):
             assemble(
                 x_ref,
@@ -172,7 +172,7 @@
 
         for e in range(3):
             side_ref[e, 0:9] = x_ref[e, 0:9]
-            side_ref[e, 9:18] = x_ref[e, 55:64]
+            side_ref[e, 9:18] = x_ref[e, 39:48]
 
     multiply(w_ref, x_ref, step * 8 + 7, out_ref)
 
@@ -181,7 +181,7 @@
     step = pl.program_id(0)
 
     def group(g):
-        at = 8 * g + 1 + 18 * (g // 4)
+        at = 8 * g + 1 + 18 * (g // 5)
         assemble(
             x_ref,
             lambda q: recv_ref[slot_ref[q], pl.ds(g * 4, 4)] + late_ref[pl.ds(g * 4, 4), q],
@@ -190,28 +190,28 @@
             lambda p, side: at + 2 * p + side,
         )
 
-    row = 8 * step + 2 * (step // 5)
+    row = 8 * step + 2 * (step // 6)
 
     @pl.when(step == 0)
     def _():
-        place_early(late_ref, lambda q, h: recv_ref[slot_ref[q], 33 + h], spread_ref)
+        place_early(late_ref, lambda q, h: recv_ref[slot_ref[q], 41 + h], spread_ref)
         for e in range(3):
-            x_ref[e, 33:51] = side_ref[e]
+            x_ref[e, 41:59] = side_ref[e]
         assemble(
             x_ref,
-            lambda q: recv_ref[slot_ref[q], 32] + late_ref[32, q],
+            lambda q: recv_ref[slot_ref[q], 40] + late_ref[40, q],
             1,
             (0, 1),
-            lambda p, side: 83 * side,
+            lambda p, side: 99 * side,
         )
         group(0)
 
-    @pl.when(step < 7)
+    @pl.when(step < 9)
     def _():
         group(step + 1)
         multiply(w_ref, x_ref, row, out_ref)
 
-    @pl.when(step >= 7)
+    @pl.when(step >= 9)
     def _():
         multiply(w_ref, x_ref, row, out_ref)
 
@@ -237,7 +237,7 @@
     got = ([], [])
     for step in (0, 1):
         rows = lax.dynamic_slice_in_dim(waveform, 256 * (step ^ z2), 256, 0)
-        part = rows.reshape(2, 128, 16, HOP)[:, 32:96]
+        part = rows.reshape(2, 128, 16, HOP)[:, 40:88]
         got[0].append(send(part, bulk_route(step)))
     up = [(i, i + 1) for i in range(7)]
     row_low = send(waveform[511:], up, "fiber")
@@ -249,7 +249,7 @@
         rows = lax.dynamic_slice_in_dim(wave, 256 * (step ^ z2), 256, 0)
         rows = rows.reshape(2, 128, 16, HOP)
         extra = lax.dynamic_slice_in_dim(sides, 2 * (step ^ z2), 2, 0)
-        part = jnp.concatenate([rows[:, :32], rows[:, 96:], extra], axis=1)
+        part = jnp.concatenate([rows[:, :40], rows[:, 88:], extra], axis=1)
         got[1].append(send(part, bulk_route(step)))
 
     taps = pl.pallas_call(
@@ -263,7 +263,7 @@
     where = jnp.stack([first, core, keep]).astype(jnp.int32)
     recv = []
     for half in (0, 1):
-        size = 66 if half else 64
+        size = 82 if half else 48
         theirs = [lax.dynamic_index_in_dim(g, 1 - core, 0, False) for g in got[half]]
         other = send(jnp.stack(theirs), OTHER_CORE, "tm")
         feats = pl.pallas_call(
@@ -324,17 +324,17 @@
         ),
         grid_spec=pltpu.PrefetchScalarGridSpec(
             num_scalar_prefetch=1,
-            grid=(6,),
+            grid=(4,),
             in_specs=[
-                whole(8, 34, GW, 128),
+                whole(8, 26, GW, 128),
                 whole(128, 21 * 128),
-                pl.BlockSpec((1, 256, 960), lambda i, s: (i + 5, 0, 0)),
+                pl.BlockSpec((1, 256, 960), lambda i, s: (i + 6, 0, 0)),
             ],
             out_specs=(
-                pl.BlockSpec((8, GW, 512), lambda i, s: (i + 5, 0, 0)),
+                pl.BlockSpec((8, GW, 512), lambda i, s: (i + 6, 0, 0)),
                 whole(3, 18, GW, 512),
             ),
-            scratch_shapes=[pltpu.VMEM((3, 64, GW, 512), jnp.bfloat16), late_rows],
+            scratch_shapes=[pltpu.VMEM((3, 48, GW, 512), jnp.bfloat16), late_rows],
         ),
         cost_estimate=pl.CostEstimate(
             flops=6 * 2 * 256 * 960 * 512, bytes_accessed=8 << 20, transcendentals=0
@@ -346,16 +346,16 @@
         out_shape=jax.ShapeDtypeStruct((128, GW, 512), jnp.bfloat16),
         grid_spec=pltpu.PrefetchScalarGridSpec(
             num_scalar_prefetch=1,
-            grid=(10,),
+            grid=(12,),
             in_specs=[
-                whole(8, 35, GW, 128),
+                whole(8, 43, GW, 128),
                 whole(128, 21 * 128),
                 whole(3, 18, GW, 512),
-                pl.BlockSpec((1, 256, 960), lambda i, s: (i + 6 * (i // 5), 0, 0)),
+                pl.BlockSpec((1, 256, 960), lambda i, s: (i + 4 * (i // 6), 0, 0)),
                 pl.BlockSpec(memory_space=pl.ANY),
             ],
-            out_specs=pl.BlockSpec((8, GW, 512), lambda i, s: (i + 6 * (i // 5), 0, 0)),
-            scratch_shapes=[pltpu.VMEM((3, 84, GW, 512), jnp.bfloat16), late_rows],
+            out_specs=pl.BlockSpec((8, GW, 512), lambda i, s: (i + 4 * (i // 6), 0, 0)),
+            scratch_shapes=[pltpu.VMEM((3, 100, GW, 512), jnp.bfloat16), late_rows],
         ),
         input_output_aliases={5: 0},
         cost_estimate=pl.CostEstimate(

time: 173 us -> 183 us (1.058)
  the two profiles are of different devices: /device:TPU:16 before, /device:TPU:152 now
where the time goes in v3:
time: 183 us; the launch traced here: 182 us
  waiting for transfers between devices  73.8 us (40%)
  starting transfers between devices  51.3 us (28%)
  Pallas kernels  46 us (25%)
  local copies, waits for them, and re-layouts  7.66 us (4%)
  other arithmetic  3.35 us (2%)
    ppermute x8, waiting for transfers between devices, send(): return lax.ppermute(part, axes, perm)  61.4 us
    all_to_all x2, starting transfers between devices, shards(): recv.append(lax.all_to_all(feats, 'fiber', 0, 0, tiled=True))  31.7 us
    ppermute x8, starting transfers between devices, send(): return lax.ppermute(part, axes, perm)  19.6 us
    pallas_call x1, Pallas kernels, shards(): pl.pallas_call(outer_kernel, out_shape=jax.ShapeDtypeStruct((128, GW, 512...  16.3 us
    all_to_all x2, waiting for transfers between devices, shards(): recv.append(lax.all_to_all(feats, 'fiber', 0, 0, tiled=True))  12.4 us
    pallas_call x1, Pallas kernels, shards(): pl.pallas_call(weight_kernel, out_shape=jax.ShapeDtypeStruct((16, 256, 96...  9.55 us
    pallas_call x1, Pallas kernels, shards(): pl.pallas_call(inner_kernel, out_shape=(jax.ShapeDtypeStruct((128, GW, 51...  9.47 us
    pallas_call x2, Pallas kernels, shards(): pl.pallas_call(filter_kernel, out_shape=jax.ShapeDtypeStruct((8, size //...  8.93 us
  transfers between devices with their start and end apart: 10, of which 6 were waited for; matrix products, arithmetic and copies ran while one was open for 4% of the time, Pallas kernels for 14%

profile of v3, /device:TPU:152, one launch (start us, length us, event | category | flops | bytes accessed | tf_op | source)
XLA Modules:
  0.0 182.4 jit_solution(664354747589821566)
XLA Ops:
  0.0 0.0 copy-start
  0.0 1.7 dynamic-slice_bitcast_fusion
  1.7 0.2 copy.19
  2.0 0.1 collective-permute-start.6
  2.1 0.0 copy-start.2
  2.1 0.2 copy.18
  2.3 0.8 slice.72
  3.1 7.6 %collective-permute-start.5 = (bf16[2,48,16,128]{3,2,1,0:T(8,128)(2,1)}, bf16[2,48,16,128]{3,2,1,0:T(8,128)(2,1)S(1)}, u32[]{:S(2)}, u32[]{:S(2)}) collective-permute-start(bf16[2,48,16,128]{3,2,1,0:T(8,128)(2,1)} %slice.72), channel_id=1, source_target_pairs={{0,0},{8,8},{1,33},{9,41},{16,1},{24,9},{17,32},{25,40},{32,17},{4... | collective-permute-start | bytes 1179656 | tf_op jit(solution)/shard_map/ppermute | solution.py:235
  10.7 4.3 %collective-permute-done.6.second_ref = bf16[2,48,16,128]{3,2,1,0:T(8,128)(2,1)S(1)} collective-permute-done((bf16[2,48,16,128]{3,2,1,0:T(8,128)(2,1)S(1)}, bf16[2,48,16,128]{3,2,1,0:T(8,128)(2,1)S(1)}, u32[]{:S(2)}, u32[]{:S(2)}) %collective-permute-start.6) | collective-permute-done | bytes 393248 | tf_op jit(solution)/shard_map/ppermute | solution.py:235
  15.0 0.0 copy-start.5
  15.0 10.5 %collective-permute-done.5.first_ref = bf16[2,48,16,128]{3,2,1,0:T(8,128)(2,1)S(1)} collective-permute-done((bf16[2,48,16,128]{3,2,1,0:T(8,128)(2,1)}, bf16[2,48,16,128]{3,2,1,0:T(8,128)(2,1)S(1)}, u32[]{:S(2)}, u32[]{:S(2)}) %collective-permute-start.5) | collective-permute-done | bytes 393248 | tf_op jit(solution)/shard_map/ppermute | solution.py:235
  25.6 0.0 copy-start.6
  25.6 0.1 collective-permute-start.7
  25.7 0.0 copy-done.2
  25.8 1.3 collective-permute-start.1
  27.1 4.5 %collective-permute-start = (bf16[1,2048]{1,0:T(2,128)(2,1)S(1)}, bf16[1,2048]{1,0:T(2,128)(2,1)S(1)}, u32[]{:S(2)}, u32[]{:S(2)}) collective-permute-start(bf16[1,2048]{1,0:T(2,128)(2,1)S(1)} %get-tuple-element.26), channel_id=1, source_target_pairs={{0,1},{1,2},{2,3},{3,4},{4,5},{5,6},{6,7},{8,9},{9,10},{10,11},{11... | collective-permute-start | bytes 12296 | tf_op jit(solution)/shard_map/ppermute | solution.py:235
  31.6 0.6 pad_add_fusion.1.where_ref
  32.2 1.8 flip.1.taps_ref
  34.0 0.0 collective-permute-done.1
  34.0 0.0 collective-permute-done
  34.0 0.0 collective-permute-done.7.other_ref
  34.0 0.0 copy-done.5
  34.0 0.0 copy-done.6
  34.0 3.8 %filterbank.3 = bf16[8,26,32,128]{3,2,1,0:T(8,128)(2,1)} custom-call(s32[3]{0:T(128)} %pad_add_fusion.1.where_ref, bf16[2,48,16,128]{3,2,1,0:T(8,128)(2,1)} %copy-done.6, bf16[2,48,16,128]{3,2,1,0:T(8,128)(2,1)} %copy-done.5, bf16[2,48,16,128]{3,2,1,0:T(8,128)(2,1)} %collective-permute-done.7.other_ref, bf16[256,512]{1,0:T(8,128)(2,1)} %flip.1.taps_ref), custom_call_target="tpu_custom_call" | custom-call | flops 805306368 | bytes 2359296 | tf_op jit(solution)/shard_map/filterbank/pallas_call | solution.py:269
  37.8 9.4 %all-to-all-start.1 = ((bf16[8,26,32,128]{3,2,1,0:T(8,128)(2,1)}), bf16[8,26,32,128]{3,2,1,0:T(8,128)(2,1)}, u32[]{:S(2)}, u32[]{:S(2)}) async-start(bf16[8,26,32,128]{3,2,1,0:T(8,128)(2,1)} %filterbank.3), calls=%async_computation.1 | async-start | bytes 3407872 | tf_op jit(solution)/shard_map/all_to_all | solution.py:283
  47.2 0.1 concatenate.12
  47.4 0.1 dynamic-slice_bitcast_fusion.2
  47.5 0.2 copy.17
  47.8 0.1 fusion.30
  47.9 0.1 pad_maximum_fusion.1
  48.0 0.7 collective-permute-start.3
  48.7 0.2 copy.15
  48.9 0.1 fusion.31
  49.0 0.1 pad_maximum_fusion
  49.1 5.2 %collective-permute-start.2 = (bf16[2,82,16,128]{3,2,1,0:T(8,128)(2,1)S(1)}, bf16[2,82,16,128]{3,2,1,0:T(8,128)(2,1)S(1)}, u32[]{:S(2)}, u32[]{:S(2)}) collective-permute-start(bf16[2,82,16,128]{3,2,1,0:T(8,128)(2,1)S(1)} %pad_maximum_fusion), channel_id=1, source_target_pairs={{0,0},{8,8},{1,33},{9,41},{16,1},{24,9},{17,32},{25,40},{32,17},{4... | collective-permute-start | bytes 2015240 | tf_op jit(solution)/shard_map/ppermute | solution.py:235
  54.4 43.8 %collective-permute-done.3.second_ref = bf16[2,82,16,128]{3,2,1,0:T(8,128)(2,1)S(1)} collective-permute-done((bf16[2,82,16,128]{3,2,1,0:T(8,128)(2,1)S(1)}, bf16[2,82,16,128]{3,2,1,0:T(8,128)(2,1)S(1)}, u32[]{:S(2)}, u32[]{:S(2)}) %collective-permute-start.3) | collective-permute-done | bytes 671776 | tf_op jit(solution)/shard_map/ppermute | solution.py:235
  98.1 0.7 collective-permute-done.2.first_ref
  98.9 0.1 pad_maximum_fusion.2
  99.0 0.1 collective-permute-start.4
  99.1 2.1 %collective-permute-done.4.other_ref = bf16[2,82,16,128]{3,2,1,0:T(8,128)(2,1)S(1)} collective-permute-done((bf16[2,82,16,128]{3,2,1,0:T(8,128)(2,1)S(1)}, bf16[2,82,16,128]{3,2,1,0:T(8,128)(2,1)S(1)}, u32[]{:S(2)}, u32[]{:S(2)}) %collective-permute-start.4) | collective-permute-done | bytes 671776 | tf_op jit(solution)/shard_map/ppermute | solution.py:235
  101.2 0.0 copy-done.3
  101.2 0.0 copy-done.4
  101.2 0.8 copy-done.7
  102.0 5.2 %filterbank.2 = bf16[8,43,32,128]{3,2,1,0:T(8,128)(2,1)} custom-call(s32[3]{0:T(128)} %pad_add_fusion.1.where_ref, bf16[2,82,16,128]{3,2,1,0:T(8,128)(2,1)} %copy-done.4, bf16[2,82,16,128]{3,2,1,0:T(8,128)(2,1)} %copy-done.3, bf16[2,82,16,128]{3,2,1,0:T(8,128)(2,1)} %copy-done.7, bf16[256,512]{1,0:T(8,128)(2,1)} %flip.1.taps_ref), custom_call_target="tpu_custom_call" | custom-call | flops 1375731712 | bytes 4030464 | tf_op jit(solution)/shard_map/filterbank/pallas_call | solution.py:269
  107.2 0.0 all-to-all-done.1.recv_ref
  107.2 22.3 %all-to-all-start = ((bf16[8,43,32,128]{3,2,1,0:T(8,128)(2,1)}), bf16[8,43,32,128]{3,2,1,0:T(8,128)(2,1)S(1)}, u32[]{:S(2)}, u32[]{:S(2)}) async-start(bf16[8,43,32,128]{3,2,1,0:T(8,128)(2,1)} %filterbank.2), calls=%async_computation | async-start | bytes 5636096 | tf_op jit(solution)/shard_map/all_to_all | solution.py:283
  129.5 0.0 copy-done.9
  129.5 0.1 concatenate.15
  129.6 0.1 dynamic_slice.48
  129.6 0.1 slice.65
  129.7 0.0 copy-done.8
  129.7 0.1 copy.13
  129.8 0.8 reshape.77.kern_ref
  130.6 0.0 copy-done
  130.6 0.2 select_reduce_fusion
  130.8 0.1 fusion.25
  130.9 0.6 pad_add_fusion.flag_ref
  131.5 9.6 %weights.1.w_ref = bf16[16,256,960]{2,1,0:T(8,128)(2,1)} custom-call(s32[3,128]{1,0:T(4,128)} %pad_add_fusion.flag_ref, bf16[64,288]{1,0:T(8,128)(2,1)} %reshape.77.kern_ref), custom_call_target="tpu_custom_call" | custom-call | flops 283115520 | bytes 8388608 | tf_op jit(solution)/shard_map/weights/pallas_call | solution.py:297
  141.0 0.6 xor_add_fusion.slot_ref
  141.6 1.0 fusion.spread_ref
  142.6 9.5 %conv_inner.1 = (bf16[128,32,512]{2,1,0:T(8,128)(2,1)}, bf16[3,18,32,512]{3,2,1,0:T(8,128)(2,1)}) custom-call(s32[8]{0:T(128)} %xor_add_fusion.slot_ref, bf16[8,26,32,128]{3,2,1,0:T(8,128)(2,1)} %all-to-all-done.1.recv_ref, bf16[128,2688]{1,0:T(8,128)(2,1)} %fusion.spread_ref, bf16[16,256,960]{2,1,0:T(8,128)(2,1)} %weights.1.w_ref), custom_call_target="tpu_custom_call" | custom-call | flops 1509949440 | bytes 8388608 | tf_op jit(solution)/shard_map/conv_inner/pallas_call | solution.py:319
  152.1 12.4 %all-to-all-done.recv_ref = bf16[8,43,32,128]{3,2,1,0:T(8,128)(2,1)S(1)} async-done(((bf16[8,43,32,128]{3,2,1,0:T(8,128)(2,1)}), bf16[8,43,32,128]{3,2,1,0:T(8,128)(2,1)S(1)}, u32[]{:S(2)}, u32[]{:S(2)}) %all-to-all-start) | async-done | bytes 2818080 | tf_op jit(solution)/shard_map/all_to_all | solution.py:283
  164.5 1.6 copy-done.1
  166.1 16.3 %conv_outer.1 = bf16[128,32,512]{2,1,0:T(8,128)(2,1)} custom-call(s32[8]{0:T(128)} %xor_add_fusion.slot_ref, bf16[8,43,32,128]{3,2,1,0:T(8,128)(2,1)} %copy-done.1, bf16[128,2688]{1,0:T(8,128)(2,1)} %fusion.spread_ref, bf16[3,18,32,512]{3,2,1,0:T(8,128)(2,1)} %get-tuple-element.13.side_ref, ...), custom_call_target="tpu_custom_call", output_to_operand_aliasing={{}: (5, {})} | custom-call | flops 2516582400 | bytes 8388608 | tf_op jit(solution)/shard_map/conv_outer/pallas_call | solution.py:344
  (18 shorter events, 0.2 us)
Async XLA Ops:
  0.0 130.6 %copy-start = (s32[128,8]{0,1:T(8,128)S(1)}, s32[128,8]{0,1:T(8,128)}, u32[]{:S(2)}) copy-start(s32[128,8]{0,1:T(8,128)} %param.9) | copy-start | bytes 12292
  2.0 13.0 %collective-permute-start.6 = (bf16[2,48,16,128]{3,2,1,0:T(8,128)(2,1)S(1)}, bf16[2,48,16,128]{3,2,1,0:T(8,128)(2,1)S(1)}, u32[]{:S(2)}, u32[]{:S(2)}) collective-permute-start(bf16[2,48,16,128]{3,2,1,0:T(8,128)(2,1)S(1)} %slice.73), channel_id=1, source_target_pairs={{0,16},{8,24},{1,49},{9,57},{16,17},{24,25},{17,48},{25,56},{32,1}... | collective-permute-start | bytes 1179656 | tf_op jit(solution)/shard_map/ppermute | solution.py:235
  2.1 23.7 %copy-start.2 = (bf16[512,2048]{1,0:T(8,128)(2,1)S(1)}, bf16[512,2048]{1,0:T(8,128)(2,1)}, u32[]{:S(2)}) copy-start(bf16[512,2048]{1,0:T(8,128)(2,1)} %param.6) | copy-start | bytes 6291460
  3.1 22.5 %collective-permute-start.5 = (bf16[2,48,16,128]{3,2,1,0:T(8,128)(2,1)}, bf16[2,48,16,128]{3,2,1,0:T(8,128)(2,1)S(1)}, u32[]{:S(2)}, u32[]{:S(2)}) collective-permute-start(bf16[2,48,16,128]{3,2,1,0:T(8,128)(2,1)} %slice.72), channel_id=1, source_target_pairs={{0,0},{8,8},{1,33},{9,41},{16,1},{24,9},{17,32},{25,40},{32,17},{4... | collective-permute-start | bytes 1179656 | tf_op jit(solution)/shard_map/ppermute | solution.py:235
  15.0 19.0 %copy-start.5 = (bf16[2,48,16,128]{3,2,1,0:T(8,128)(2,1)}, bf16[2,48,16,128]{3,2,1,0:T(8,128)(2,1)S(1)}, u32[]{:S(2)}) copy-start(bf16[2,48,16,128]{3,2,1,0:T(8,128)(2,1)S(1)} %collective-permute-done.6.second_ref) | copy-start | bytes 1179652
  25.6 8.5 %copy-start.6 = (bf16[2,48,16,128]{3,2,1,0:T(8,128)(2,1)}, bf16[2,48,16,128]{3,2,1,0:T(8,128)(2,1)S(1)}, u32[]{:S(2)}) copy-start(bf16[2,48,16,128]{3,2,1,0:T(8,128)(2,1)S(1)} %collective-permute-done.5.first_ref) | copy-start | bytes 1179652
  25.6 8.4 %collective-permute-start.7 = (bf16[2,48,16,128]{3,2,1,0:T(8,128)(2,1)S(1)}, bf16[2,48,16,128]{3,2,1,0:T(8,128)(2,1)}, u32[]{:S(2)}, u32[]{:S(2)}) collective-permute-start(bf16[2,48,16,128]{3,2,1,0:T(8,128)(2,1)S(1)} %pad_maximum_fusion.3), channel_id=1, source_target_pairs={{0,8},{8,0},{16,24},{24,16},{32,40},{40,32},{48,56},{56,48},{64,72... | collective-permute-start | bytes 1179656 | tf_op jit(solution)/shard_map/ppermute | solution.py:235
  25.8 8.3 %collective-permute-start.1 = (bf16[1,2048]{1,0:T(2,128)(2,1)S(1)}, bf16[1,2048]{1,0:T(2,128)(2,1)S(1)}, u32[]{:S(2)}, u32[]{:S(2)}) collective-permute-start(bf16[1,2048]{1,0:T(2,128)(2,1)S(1)} %get-tuple-element.25), channel_id=1, source_target_pairs={{1,0},{2,1},{3,2},{4,3},{5,4},{6,5},{7,6},{9,8},{10,9},{11,10},{12... | collective-permute-start | bytes 12296 | tf_op jit(solution)/shard_map/ppermute | solution.py:235
  27.1 7.0 %collective-permute-start = (bf16[1,2048]{1,0:T(2,128)(2,1)S(1)}, bf16[1,2048]{1,0:T(2,128)(2,1)S(1)}, u32[]{:S(2)}, u32[]{:S(2)}) collective-permute-start(bf16[1,2048]{1,0:T(2,128)(2,1)S(1)} %get-tuple-element.26), channel_id=1, source_target_pairs={{0,1},{1,2},{2,3},{3,4},{4,5},{5,6},{6,7},{8,9},{9,10},{10,11},{11... | collective-permute-start | bytes 12296 | tf_op jit(solution)/shard_map/ppermute | solution.py:235
  37.8 69.4 %all-to-all-start.1 = ((bf16[8,26,32,128]{3,2,1,0:T(8,128)(2,1)}), bf16[8,26,32,128]{3,2,1,0:T(8,128)(2,1)}, u32[]{:S(2)}, u32[]{:S(2)}) async-start(bf16[8,26,32,128]{3,2,1,0:T(8,128)(2,1)} %filterbank.3), calls=%async_computation.1 | async-start | bytes 3407872 | tf_op jit(solution)/shard_map/all_to_all | solution.py:283
  48.0 50.1 %collective-permute-start.3 = (bf16[2,82,16,128]{3,2,1,0:T(8,128)(2,1)S(1)}, bf16[2,82,16,128]{3,2,1,0:T(8,128)(2,1)S(1)}, u32[]{:S(2)}, u32[]{:S(2)}) collective-permute-start(bf16[2,82,16,128]{3,2,1,0:T(8,128)(2,1)S(1)} %pad_maximum_fusion.1), channel_id=1, source_target_pairs={{0,16},{8,24},{1,49},{9,57},{16,17},{24,25},{17,48},{25,56},{32,1}... | collective-permute-start | bytes 2015240 | tf_op jit(solution)/shard_map/ppermute | solution.py:235
  49.1 49.7 %collective-permute-start.2 = (bf16[2,82,16,128]{3,2,1,0:T(8,128)(2,1)S(1)}, bf16[2,82,16,128]{3,2,1,0:T(8,128)(2,1)S(1)}, u32[]{:S(2)}, u32[]{:S(2)}) collective-permute-start(bf16[2,82,16,128]{3,2,1,0:T(8,128)(2,1)S(1)} %pad_maximum_fusion), channel_id=1, source_target_pairs={{0,0},{8,8},{1,33},{9,41},{16,1},{24,9},{17,32},{25,40},{32,17},{4... | collective-permute-start | bytes 2015240 | tf_op jit(solution)/shard_map/ppermute | solution.py:235
  98.1 3.0 %copy-start.3 = (bf16[2,82,16,128]{3,2,1,0:T(8,128)(2,1)}, bf16[2,82,16,128]{3,2,1,0:T(8,128)(2,1)S(1)}, u32[]{:S(2)}) copy-start(bf16[2,82,16,128]{3,2,1,0:T(8,128)(2,1)S(1)} %collective-permute-done.3.second_ref) | copy-start | bytes 2015236
  98.8 2.3 %copy-start.4 = (bf16[2,82,16,128]{3,2,1,0:T(8,128)(2,1)}, bf16[2,82,16,128]{3,2,1,0:T(8,128)(2,1)S(1)}, u32[]{:S(2)}) copy-start(bf16[2,82,16,128]{3,2,1,0:T(8,128)(2,1)S(1)} %collective-permute-done.2.first_ref) | copy-start | bytes 2015236
  99.0 2.2 %collective-permute-start.4 = (bf16[2,82,16,128]{3,2,1,0:T(8,128)(2,1)S(1)}, bf16[2,82,16,128]{3,2,1,0:T(8,128)(2,1)S(1)}, u32[]{:S(2)}, u32[]{:S(2)}) collective-permute-start(bf16[2,82,16,128]{3,2,1,0:T(8,128)(2,1)S(1)} %pad_maximum_fusion.2), channel_id=1, source_target_pairs={{0,8},{8,0},{16,24},{24,16},{32,40},{40,32},{48,56},{56,48},{64,72... | collective-permute-start | bytes 2015240 | tf_op jit(solution)/shard_map/ppermute | solution.py:235
  101.2 0.8 copy-start.7
  107.2 22.3 %copy-start.9 = (s32[4096]{0:T(1024)S(1)}, s32[4096]{0:T(1024)}, u32[]{:S(2)}) copy-start(s32[4096]{0:T(1024)} %param.8) | copy-start | bytes 49156
  107.2 22.5 %copy-start.8 = (bf16[2,1,3,3,32,32]{5,4,3,2,1,0:T(8,128)(2,1)S(1)}, bf16[2,1,3,3,32,32]{5,4,3,2,1,0:T(8,128)(2,1)}, u32[]{:S(2)}) copy-start(bf16[2,1,3,3,32,32]{5,4,3,2,1,0:T(8,128)(2,1)} %param.10) | copy-start | bytes 110596
  107.2 57.3 %all-to-all-start = ((bf16[8,43,32,128]{3,2,1,0:T(8,128)(2,1)}), bf16[8,43,32,128]{3,2,1,0:T(8,128)(2,1)S(1)}, u32[]{:S(2)}, u32[]{:S(2)}) async-start(bf16[8,43,32,128]{3,2,1,0:T(8,128)(2,1)} %filterbank.2), calls=%async_computation | async-start | bytes 5636096 | tf_op jit(solution)/shard_map/all_to_all | solution.py:283
  164.5 1.6 copy-start.1
